TPU v7x, 128 devices: a whole 4x4x4 slice. The times are simulated.
128 devices in a mesh: dp: 4 (over z), ctx: 16 (over y, x_lo, core), tp: 2 (over x_hi).
Axes of the slice: x: 4 (x_hi: 2, x_lo: 2; x = x_hi * 2 + x_lo), y: 4, z: 4, core: 2. Of those that a mesh axis runs over, the one named last changes fastest.
Arguments:
- projected: bfloat16 [4, 2048, 3, 8192], P('dp', 'ctx', None, 'tp'), may hold values from -6 to 6
- upstream: bfloat16 [4, 2048, 8192], P('dp', 'ctx', 'tp'), may hold values from -6 to 6
- short_weight: float32 [3, 3, 8192], P(None, None, 'tp'), may hold values from -3.5 to 3.5
- skip_gain: float32 [8192], P('tp'), may hold values from 0.5 to 2
- residues: float32 [512, 16], replicated, may hold values from -2.5 to 2.5
- rates: float32 [512, 16], replicated, may hold values from 0.00024414062 to 0.05
Outputs:
- mixed: bfloat16 [4, 2048, 8192], P('dp', 'ctx', 'tp')
- grad_projected: bfloat16 [4, 2048, 3, 8192], P('dp', 'ctx', None, 'tp')
- grad_short: float32 [3, 3, 8192], P(None, None, 'tp')
- grad_skip: float32 [8192], P('tp')
- grad_residues: float32 [512, 16], replicated
- grad_log_rates: float32 [512, 16], replicated
All inputs are finite; a program needn't handle non-finite values.
Results may differ from a plain program's by a relative error of at most 0.007.
Values may be sent and summed in bfloat16 or wider, within the bound.
A program may use at most 192 MiB of HBM per device.

v0:
```python
import math

import jax
import jax.numpy as jnp
from jax import lax
from jax.sharding import PartitionSpec as P

GROUP = 16


PRECISE = lax.Precision.HIGHEST


def shifted(value, axis, steps):
    count = lax.axis_size(axis)
    leading, last = (max(0, -steps), min(count, count - steps))
    return lax.ppermute(value, axis, [(source, source + steps) for source in range(leading, last)])


def angles(full_size, row_count, col_count):
    left = lax.broadcasted_iota(jnp.int32, (row_count, col_count), 0)
    right = lax.broadcasted_iota(jnp.int32, (row_count, col_count), 1)
    return (left * right % full_size).astype(jnp.float32) * (2.0 * math.pi / full_size)


def spectrum(signal, radix_size):
    lead_size = signal.shape[0]
    length = signal.shape[1]
    chan_size = signal.shape[2]
    full_size = 2 * length
    outer_size = full_size // radix_size
    blocks = signal.reshape(lead_size, outer_size // 2, radix_size, chan_size)
    section_one = angles(outer_size, outer_size, outer_size // 2)
    table_one = jnp.stack([jnp.cos(section_one), -jnp.sin(section_one)], axis=0)
    first = jnp.einsum("zkm,bmpc->bzkpc", table_one, blocks, precision=PRECISE)
    twiddle = angles(full_size, outer_size, radix_size)
    cos_turn = jnp.cos(twiddle)[None, :, :, None]
    sin_turn = jnp.sin(twiddle)[None, :, :, None]
    real_one = first[:, 0]
    imag_one = first[:, 1]
    turned = jnp.stack(
        [real_one * cos_turn + imag_one * sin_turn, imag_one * cos_turn - real_one * sin_turn],
        axis=1,
    )
    section_two = angles(radix_size, radix_size, radix_size)
    cos_two = jnp.cos(section_two)
    sin_two = jnp.sin(section_two)
    table_two = jnp.stack(
        [jnp.stack([cos_two, -sin_two], axis=1), jnp.stack([sin_two, cos_two], axis=1)], axis=0
    )
    return jnp.einsum("bzkpc,zpyj->bykjc", turned, table_two, precision=PRECISE)


def inverse(stacked, radix_size):
    lead_size = stacked.shape[0]
    outer_size = stacked.shape[2]
    chan_size = stacked.shape[4]
    full_size = outer_size * radix_size
    section_two = angles(radix_size, radix_size, radix_size)
    cos_two = jnp.cos(section_two)
    sin_two = jnp.sin(section_two)
    table_two = jnp.stack(
        [jnp.stack([cos_two, sin_two], axis=1), jnp.stack([-sin_two, cos_two], axis=1)], axis=0
    )
    second = jnp.einsum("bzkjc,zjyp->bykpc", stacked, table_two, precision=PRECISE)
    twiddle = angles(full_size, outer_size, radix_size)
    cos_turn = jnp.cos(twiddle)[None, :, :, None]
    sin_turn = jnp.sin(twiddle)[None, :, :, None]
    real_two = second[:, 0]
    imag_two = second[:, 1]
    turned = jnp.stack(
        [real_two * cos_turn - imag_two * sin_turn, imag_two * cos_turn + real_two * sin_turn],
        axis=1,
    )
    section_one = angles(outer_size, outer_size // 2, outer_size)
    table_one = jnp.stack([jnp.cos(section_one), -jnp.sin(section_one)], axis=0) / full_size
    result = jnp.einsum("zmk,bzkpc->bmpc", table_one, turned, precision=PRECISE)
    return result.reshape(lead_size, full_size // 2, chan_size)


def product(signal, filt, conjugate):
    shape = signal.shape
    group_count = filt.shape[4]
    grouped = signal.reshape(
        shape[0], shape[1], shape[2], shape[3], group_count, shape[4] // group_count
    )
    real_filt = filt[:, 0][..., None]
    imag_filt = filt[:, 1][..., None]
    real_sig = grouped[:, 0]
    imag_sig = grouped[:, 1]
    if conjugate:
        real_out = real_filt * real_sig + imag_filt * imag_sig
        imag_out = real_filt * imag_sig - imag_filt * real_sig
    else:
        real_out = real_filt * real_sig - imag_filt * imag_sig
        imag_out = real_filt * imag_sig + imag_filt * real_sig
    return jnp.stack([real_out, imag_out], axis=1).reshape(shape)


def local(projected, upstream, short_weight, skip_gain, residues, rates):
    slab_count = projected.shape[0]
    tok_rows = projected.shape[1]
    half_width = projected.shape[3]
    tap_count = short_weight.shape[1]
    ctx_count = lax.axis_size("ctx")
    dp_count = lax.axis_size("dp")
    chan_width = half_width // ctx_count
    group_count = chan_width // GROUP
    length = tok_rows * ctx_count
    radix_size = math.gcd(length, 128)
    before = shifted(projected[:, tok_rows - (tap_count - 1) :], "ctx", 1)
    padded = jnp.concatenate([before, projected], axis=1).astype(jnp.float32)
    features = jnp.zeros(projected.shape, jnp.float32)
    for offset in range(tap_count):
        start_row = tap_count - 1 - offset
        features = (
            features + padded[:, start_row : start_row + tok_rows] * short_weight[:, offset, :]
        )
    query_part = features[:, :, 0]
    key_part = features[:, :, 1]
    value_part = features[:, :, 2]
    gated = (key_part * value_part).astype(jnp.bfloat16)
    gated_wide = gated.astype(jnp.float32)
    upstream_wide = upstream.astype(jnp.float32)
    grad_sum = upstream_wide * query_part
    grad_conv = grad_sum.astype(jnp.bfloat16)
    gated_blocks = gated.reshape(slab_count, tok_rows, ctx_count, chan_width)
    grad_blocks = grad_conv.reshape(slab_count, tok_rows, ctx_count, chan_width)
    group_start = (lax.axis_index("tp") * half_width + lax.axis_index("ctx") * chan_width) // GROUP
    my_residues = lax.dynamic_slice_in_dim(residues, group_start, group_count, 0)
    my_rates = lax.dynamic_slice_in_dim(rates, group_start, group_count, 0)
    positions = jnp.arange(length, dtype=jnp.float32)
    decays = jnp.exp(-(my_rates[None, :, :] * positions[:, None, None]))
    taps_out = jnp.sum(decays * (my_residues * jnp.sqrt(my_rates))[None, :, :], axis=2)
    filter_freq = spectrum(taps_out[None], radix_size)

    def to_wide(piece):
        return piece.reshape(piece.shape[0], piece.shape[1], piece.shape[3]).astype(jnp.float32)

    def to_narrow(signal):
        return signal.astype(jnp.bfloat16).reshape(
            signal.shape[0], signal.shape[1], 1, signal.shape[2]
        )

    gated_freq = spectrum(
        to_wide(lax.all_to_all(gated_blocks, "ctx", split_axis=2, concat_axis=1, tiled=True)),
        radix_size,
    )
    grad_freq = spectrum(
        to_wide(lax.all_to_all(grad_blocks, "ctx", split_axis=2, concat_axis=1, tiled=True)),
        radix_size,
    )
    convolved = inverse(product(gated_freq, filter_freq, False), radix_size)
    correlated = inverse(product(grad_freq, filter_freq, True), radix_size)
    conv_tok = lax.all_to_all(to_narrow(convolved), "ctx", split_axis=1, concat_axis=2, tiled=True)
    corr_tok = lax.all_to_all(to_narrow(correlated), "ctx", split_axis=1, concat_axis=2, tiled=True)
    real_g = gated_freq[:, 0]
    imag_g = gated_freq[:, 1]
    real_d = grad_freq[:, 0]
    imag_d = grad_freq[:, 1]
    cross = jnp.stack(
        [real_g * real_d + imag_g * imag_d, real_g * imag_d - imag_g * real_d], axis=1
    )
    shape = cross.shape
    grouped = jnp.sum(
        cross.reshape(shape[0], shape[1], shape[2], shape[3], group_count, GROUP), axis=5
    )
    filter_grad = inverse(grouped, radix_size)
    convolved = conv_tok.reshape(slab_count, tok_rows, half_width).astype(jnp.float32)
    correlated = corr_tok.reshape(slab_count, tok_rows, half_width).astype(jnp.float32)
    mixture = convolved + skip_gain * gated_wide
    mixed = (query_part * mixture).astype(jnp.bfloat16)
    grad_query = upstream_wide * mixture
    grad_gate = correlated + skip_gain * grad_sum
    grad_rows = jnp.stack([grad_query, grad_gate * value_part, grad_gate * key_part], axis=2)
    after = shifted(grad_rows[:, : tap_count - 1], "ctx", -1)
    extended = jnp.concatenate([grad_rows, after], axis=1)
    grad_input = jnp.zeros(grad_rows.shape, jnp.float32)
    short_terms = []
    for offset in range(tap_count):
        grad_input = (
            grad_input + extended[:, offset : offset + tok_rows] * short_weight[:, offset, :]
        )
        start_row = tap_count - 1 - offset
        short_terms.append(
            jnp.sum(grad_rows * padded[:, start_row : start_row + tok_rows], axis=(0, 1))
        )
    grad_projected = grad_input.astype(jnp.bfloat16)
    norm_scale = 1.0 / math.sqrt(slab_count * dp_count * length)
    short_local = jnp.stack(short_terms, axis=1) * norm_scale
    skip_local = jnp.sum(grad_sum * gated_wide, axis=(0, 1)) * norm_scale
    grad_short, grad_skip = lax.psum((short_local, skip_local), ("dp", "ctx"))
    grad_total = jnp.sum(filter_grad, axis=0)
    sum_plain = jnp.einsum("sg,sgn->gn", grad_total, decays, precision=PRECISE)
    sum_weighted = jnp.einsum(
        "sg,sgn->gn", grad_total * positions[:, None], decays, precision=PRECISE
    )
    rate_root = jnp.sqrt(my_rates)
    residue_local = rate_root * sum_plain * norm_scale
    log_local = (
        my_residues
        * (0.5 * rate_root * sum_plain - my_rates * rate_root * sum_weighted)
        * norm_scale
    )
    empty_table = jnp.zeros(residues.shape, jnp.float32)
    residue_full = lax.dynamic_update_slice_in_dim(empty_table, residue_local, group_start, 0)
    log_full = lax.dynamic_update_slice_in_dim(empty_table, log_local, group_start, 0)
    grad_residues, grad_log_rates = lax.psum((residue_full, log_full), ("dp", "ctx", "tp"))
    return (mixed, grad_projected, grad_short, grad_skip, grad_residues, grad_log_rates)


def solution(mesh):
    in_specs = (
        P("dp", "ctx", None, "tp"),
        P("dp", "ctx", "tp"),
        P(None, None, "tp"),
        P("tp"),
        P(),
        P(),
    )
    out_specs = (
        P("dp", "ctx", "tp"),
        P("dp", "ctx", None, "tp"),
        P(None, None, "tp"),
        P("tp"),
        P(),
        P(),
    )
    return jax.shard_map(local, mesh=mesh, in_specs=in_specs, out_specs=out_specs, check_vma=False)
```

profile of v0, /device:TPU:1, one launch (start us, length us, event | category | flops | bytes accessed | tf_op | source)
XLA Modules:
  0.0 1056.9 jit_solution(9878695607234767571)
XLA Ops:
  8.2 4.5 collective-permute-start
  16.3 4.6 copy.141
  24.6 5.0 maximum_convert_fusion
  29.6 9.4 multiply_add_fusion
  43.0 5.3 all-to-all-start.2
  53.6 10.3 all-to-all-done.2
  64.0 4.7 all-to-all-start
  72.8 5.7 convolution_bitcast_fusion
  78.5 5.8 all-to-all-done
  84.3 4.4 convolution_bitcast_fusion.1
  97.5 13.2 %fusion.21 = f32[1,2,32,128,256]{4,3,2,1,0:T(8,128)} fusion(f32[2,32,128,256]{3,1,0,2:T(8,128)S(1)} %maximum_bitcast_fusion, f32[1,128,2,128]{3,1,0,2:T(8,128)S(1)} %get-tuple-element.78, f32[1,128,2,128]{3,1,0,2:T(8,128)S(1)} %copy-done.9), kind=kOutput, calls=%fused_computation.53 | convolution fusion | flops 6442516480 | bytes 17039360 | tf_op jit(solution)/shard_map/bzkpc,zpyj->bykjc/dot_general | solution.py:51
  110.7 13.0 %fusion.24 = f32[1,2,32,128,256]{4,3,2,1,0:T(8,128)} fusion(f32[2,32,128,256]{3,1,0,2:T(8,128)S(1)} %maximum_bitcast_fusion.5, f32[1,128,2,128]{3,1,0,2:T(8,128)S(1)} %get-tuple-element.78, f32[1,128,2,128]{3,1,0,2:T(8,128)S(1)} %copy-done.9), kind=kOutput, calls=%fused_computation.54 | convolution fusion | flops 6442516480 | bytes 17039360 | tf_op jit(solution)/shard_map/bzkpc,zpyj->bykjc/dot_general | solution.py:51
  123.7 8.9 copy.152
  132.6 9.9 multiply_add_fusion.1
  142.5 9.3 copy.167
  151.7 5.6 copy.178
  157.3 5.6 copy.179
  163.0 5.1 maximum_reduce_fusion
  170.7 9.2 multiply_add_fusion.3
  180.0 5.6 copy.154
  185.6 5.6 copy.155
  191.2 10.5 fusion.28
  201.7 8.1 copy.265
  209.7 5.6 copy.168
  215.4 5.7 copy.169
  221.0 10.5 fusion.27
  231.6 4.9 copy.264
  236.5 8.8 multiply_subtract_fusion.1
  245.3 4.5 fusion.37
  250.1 11.7 %copy.268 = bf16[1,2048,1,256]{3,2,0,1:T(2,128)(2,1)S(1)} copy(bf16[1,2048,1,256]{3,1,2,0:T(8,128)(2,1)S(1)} %bitcast.317) | data formatting | bytes 2097152 | tf_op jit(solution)/shard_map/convert_element_type | solution.py:141
  262.4 12.0 %reduce.2 = bf16[2048,256]{1,0:T(8,128)(2,1)} reduce(bf16[2048,1,1,256]{3,2,1,0:T(2,128)(2,1)S(1)} %bitcast.313, bf16[]{:T(256)} %broadcast.541), dimensions={1,2}, to_apply=%bitcast.296.reduce_sub_computation | reduce | bytes 2097154
  276.5 5.0 all-to-all-start.1
  281.5 6.9 fusion.38
  288.8 11.7 %copy.267 = bf16[1,2048,1,256]{3,2,0,1:T(2,128)(2,1)S(1)} copy(bf16[1,2048,1,256]{3,1,2,0:T(8,128)(2,1)S(1)} %bitcast.318) | data formatting | bytes 2097152 | tf_op jit(solution)/shard_map/convert_element_type | solution.py:141
  300.6 11.6 %reduce.1 = bf16[2048,256]{1,0:T(8,128)(2,1)} reduce(bf16[2048,1,1,256]{3,2,1,0:T(2,128)(2,1)S(1)} %bitcast.314, bf16[]{:T(256)} %broadcast.541), dimensions={1,2}, to_apply=%bitcast.295.reduce_sub_computation | reduce | bytes 2097154
  315.6 5.8 all-to-all-start.3
  324.9 4.5 reshape.804
  331.6 5.6 all-to-all-done.3
  337.2 4.3 reshape.806
  343.8 4.3 fusion.33
  354.8 4.4 copy.176
  365.1 3.9 copy.177
  369.1 10.8 %pad_maximum_fusion = f32[1,130,3,4096]{1,3,2,0:T(8,128)} fusion(f32[1,2,3,4096]{1,3,2,0:T(8,128)} %copy.177, f32[1,128,1,4096]{1,3,2,0:T(8,128)} %copy-done.2, f32[1,128,1,4096]{1,3,2,0:T(8,128)S(1)} %get-tuple-element.41, f32[1,128,1,4096]{1,3,2,0:T(8,128)} %copy-done.4), kind=kLoop, calls=%fused_computation | loop fusion | flops 4792320 | bytes 12779520 | tf_op jit(solution)/shard_map/concatenate | solution.py:177
  379.9 24.9 %multiply_reduce_fusion.2 = (f32[3,4096]{1,0:T(4,128)S(1)}, f32[3,4096]{1,0:T(4,128)S(1)}, f32[3,4096]{1,0:T(4,128)S(1)}, bf16[1,128,3,4096]{1,3,2,0:T(8,128)(2,1)}) fusion(f32[1,130,3,4096]{1,3,2,0:T(8,128)} %copy-done, f32[1,128,1,4096]{1,3,2,0:T(8,128)S(1)} %copy-done.3, f32[1,128,1,4096]{1,3,2,0:T(8,128)S(1)} %get-tuple-element.41, ...), kind=kLoop, calls=%fused_computation.37 | loop fusion | flops 21983232 | bytes 41189376 | tf_op jit(solution)/shard_map/reduce_sum | solution.py:186
  409.1 272.3 %psum.29 = f32[4096]{0:T(1024)} all-reduce(f32[4096]{0:T(1024)S(1)} %broadcast_multiply_fusion), channel_id=1, replica_groups=mesh['dp'=4,'ctx'=16,'tp'=2] {'dp','ctx'}, use_global_device_ids=true, to_apply=%region_6.7 | all-reduce | flops 4096 | bytes 32768 | tf_op jit(solution)/shard_map/psum | solution.py:192
  681.4 4.6 copy.184
  686.0 215.6 %all-reduce.4.cloned.1.call-done = f32[3,3,4096]{2,0,1:T(4,128)} async-done(((f32[3,3,4096]{2,0,1:T(4,128)}), f32[3,3,4096]{2,0,1:T(4,128)}) %all-reduce.4.cloned.1.call-update) | async-done | bytes 147472 | tf_op jit(solution)/shard_map/psum | solution.py:192
  903.4 143.7 %all-reduce.6.cloned.1.call-done = (f32[512,16]{0,1:T(8,128)}, f32[512,16]{0,1:T(8,128)}) async-done(((f32[512,16]{0,1:T(8,128)}, f32[512,16]{0,1:T(8,128)}), (f32[512,16]{0,1:T(8,128)}, f32[512,16]{0,1:T(8,128)})) %all-reduce.6.cloned.1.call-update) | async-done | bytes 65552 | tf_op jit(solution)/shard_map/psum | solution.py:208
  (151 shorter events, 68.9 us)
Async XLA Ops:
  7.2 13.8 %copy-start.12 = (bf16[1,128,4096]{2,1,0:T(8,128)(2,1)S(1)}, bf16[1,128,4096]{2,1,0:T(8,128)(2,1)}, u32[]{:S(2)}) copy-start(bf16[1,128,4096]{2,1,0:T(8,128)(2,1)} %param.7) | copy-start | bytes 3145732
  8.2 13.5 %collective-permute-start = (bf16[1,2,3,4096]{3,1,2,0:T(2,128)(2,1)S(1)}, bf16[1,2,3,4096]{3,1,2,0:T(2,128)(2,1)S(1)}, u32[]{:S(2)}, u32[]{:S(2)}) collective-permute-start(bf16[1,2,3,4096]{3,1,2,0:T(2,128)(2,1)S(1)} %slice.113), channel_id=1, source_target_pairs={{0,2},{2,4},{4,6},{6,8},{8,10},{10,12},{12,14},{14,16},{16,18},{18... | collective-permute-start | bytes 147464 | tf_op jit(solution)/shard_map/ppermute | solution.py:17
  14.9 6.1 copy-start.32
  14.9 6.8 copy-start.35
  15.1 14.5 %copy-start.14 = (f32[3,4096]{1,0:T(4,128)}, f32[3,4096]{1,0:T(4,128)S(1)}, u32[]{:S(2)}) copy-start(f32[3,4096]{1,0:T(4,128)S(1)} %get-tuple-element.87) | copy-start | bytes 147460
  15.1 14.5 %copy-start.16 = (f32[3,4096]{1,0:T(4,128)}, f32[3,4096]{1,0:T(4,128)S(1)}, u32[]{:S(2)}) copy-start(f32[3,4096]{1,0:T(4,128)S(1)} %get-tuple-element.88) | copy-start | bytes 147460
  21.0 8.6 copy-start.18
  29.6 9.5 copy-start
  39.1 2.6 copy-start.1
  43.0 20.9 %all-to-all-start.2 = ((bf16[1,128,16,256]{3,1,0,2:T(8,128)(2,1)}), bf16[1,128,16,256]{3,1,0,2:T(8,128)(2,1)S(1)}, u32[]{:S(2)}, u32[]{:S(2)}) async-start(bf16[1,128,16,256]{3,1,0,2:T(8,128)(2,1)} %copy.163), calls=%async_computation.2 | async-start | bytes 2097152 | tf_op jit(solution)/shard_map/all_to_all | solution.py:150
  48.4 1.4 copy-start.24
  64.0 20.3 %all-to-all-start = ((bf16[1,128,16,256]{3,1,0,2:T(8,128)(2,1)}), bf16[1,128,16,256]{3,1,0,2:T(8,128)(2,1)S(1)}, u32[]{:S(2)}, u32[]{:S(2)}) async-start(bf16[1,128,16,256]{3,1,0,2:T(8,128)(2,1)} %copy.146), calls=%async_computation | async-start | bytes 2097152 | tf_op jit(solution)/shard_map/all_to_all | solution.py:146
  68.7 4.1 copy-start.28
  68.7 4.1 copy-start.29
  84.3 4.4 copy-start.6
  84.3 4.4 copy-start.20
  84.3 4.4 copy-start.22
  93.9 3.5 copy-start.9
  157.3 10.7 %copy-start.11 = (f32[2,128,2,128]{3,1,2,0:T(8,128)S(1)}, f32[2,128,2,128]{3,1,2,0:T(8,128)}, u32[]{:S(2)}) copy-start(f32[2,128,2,128]{3,1,2,0:T(8,128)} %get-tuple-element.68) | copy-start | bytes 786436
  163.0 7.7 slice-start
  163.0 5.8 copy-start.10
  163.0 5.8 copy-start.25
  163.0 7.8 slice-start.1
  231.6 4.9 copy-start.21
  231.6 4.9 copy-start.23
  236.5 8.8 copy-start.26
  236.5 8.8 copy-start.27
  276.5 39.1 %all-to-all-start.1 = ((bf16[16,2,16384]{2,1,0:T(2,128)(2,1)}), bf16[16,2,16384]{2,1,0:T(2,128)(2,1)}, u32[]{:S(2)}, u32[]{:S(2)}) async-start(bf16[16,2,16384]{2,1,0:T(2,128)(2,1)} %reshape.803), calls=%async_computation.1 | async-start | bytes 2097152 | tf_op jit(solution)/shard_map/all_to_all | solution.py:155
  288.8 25.5 %copy-start.13 = (f32[1,1,32,128,16]{3,2,1,4,0:T(8,128)S(1)}, f32[1,1,32,128,16]{3,2,1,4,0:T(8,128)}, u32[]{:S(2)}) copy-start(f32[1,1,32,128,16]{3,2,1,4,0:T(8,128)} %get-tuple-element.60) | copy-start | bytes 786436
  315.6 21.6 %all-to-all-start.3 = ((bf16[16,2,16384]{2,1,0:T(2,128)(2,1)}), bf16[16,2,16384]{2,1,0:T(2,128)(2,1)}, u32[]{:S(2)}, u32[]{:S(2)}) async-start(bf16[16,2,16384]{2,1,0:T(2,128)(2,1)} %reshape.805), calls=%async_computation.3 | async-start | bytes 2097152 | tf_op jit(solution)/shard_map/all_to_all | solution.py:156
  321.4 580.2 %all-reduce.4.cloned.1.call-start = ((), (), s32[]{:S(2)}) async-start(), calls=%async_computation.4 | async-start | bytes 393216 | tf_op jit(solution)/shard_map/psum | solution.py:192
  341.7 2.1 copy-start.34
  343.8 4.3 copy-start.7
  348.0 3.5 copy-start.2
  351.5 3.2 copy-start.4
  354.8 7.3 copy-start.36
  359.2 5.9 collective-permute-start.1
  369.1 10.8 %copy-start.3 = (f32[1,128,1,4096]{1,3,2,0:T(8,128)S(1)}, f32[1,128,1,4096]{1,3,2,0:T(8,128)}, u32[]{:S(2)}) copy-start(f32[1,128,1,4096]{1,3,2,0:T(8,128)} %copy-done.2) | copy-start | bytes 6291460
  369.1 10.8 %copy-start.5 = (f32[1,128,1,4096]{1,3,2,0:T(8,128)S(1)}, f32[1,128,1,4096]{1,3,2,0:T(8,128)}, u32[]{:S(2)}) copy-start(f32[1,128,1,4096]{1,3,2,0:T(8,128)} %copy-done.4) | copy-start | bytes 6291460
  369.1 10.8 %copy-start.15 = (f32[3,4096]{1,0:T(4,128)S(1)}, f32[3,4096]{1,0:T(4,128)}, u32[]{:S(2)}) copy-start(f32[3,4096]{1,0:T(4,128)} %copy-done.14) | copy-start | bytes 147460
  369.1 10.8 %copy-start.17 = (f32[3,4096]{1,0:T(4,128)S(1)}, f32[3,4096]{1,0:T(4,128)}, u32[]{:S(2)}) copy-start(f32[3,4096]{1,0:T(4,128)} %copy-done.16) | copy-start | bytes 147460
  369.1 10.8 %copy-start.19 = (f32[3,1,4096]{2,0,1:T(4,128)S(1)}, f32[3,1,4096]{2,0,1:T(4,128)}, u32[]{:S(2)}) copy-start(f32[3,1,4096]{2,0,1:T(4,128)} %copy-done.18) | copy-start | bytes 147460
  379.9 25.7 %copy-start.33 = (f32[16,16]{0,1:T(8,128)S(1)}, f32[16,16]{0,1:T(8,128)}, u32[]{:S(2)}) copy-start(f32[16,16]{0,1:T(8,128)} %copy-done.32) | copy-start | bytes 3076
  379.9 27.9 %copy-start.8 = (bf16[1,128,4096]{1,2,0:T(8,128)(2,1)S(1)}, bf16[1,128,4096]{1,2,0:T(8,128)(2,1)}, u32[]{:S(2)}) copy-start(bf16[1,128,4096]{1,2,0:T(8,128)(2,1)} %get-tuple-element.59) | copy-start | bytes 3145732
  405.6 641.5 %all-reduce.6.cloned.1.call-start = ((), (), s32[]{:S(2)}) async-start(), calls=%async_computation.5 | async-start | bytes 131072 | tf_op jit(solution)/shard_map/psum | solution.py:208
  406.8 0.6 copy-start.31
  407.1 0.6 copy-start.30
Sparse Core Ops, SparseCore 0:
  405.7 495.9 all-reduce.3
  907.3 139.8 all-reduce.5
where the time goes:
time: 1060 us
  waiting for transfers between devices  381 us (36%)
  blocking collectives  272 us (26%)
  local copies, waits for them, and re-layouts  144 us (14%)
  other arithmetic  137 us (13%)
  matrix products  78.9 us (7%)
  starting transfers between devices  28.2 us (3%)
  between operations  15 us (1%)
    psum x1, blocking collectives, local(): grad_short, grad_skip = lax.psum((short_local, skip_local), ('dp', 'ctx'))  272 us
    psum x1, waiting for transfers between devices, local(): grad_short, grad_skip = lax.psum((short_local, skip_local), ('dp', 'ctx'))  216 us
    psum x1, waiting for transfers between devices, local(): lax.psum((residue_full, log_full), ('dp', 'ctx', 'tp'))  144 us
    unnamed x93, local copies, waits for them, and re-layouts  32.5 us
    dot_general x3, matrix products, spectrum(): return jnp.einsum('bzkpc,zpyj->bykjc', turned, table_two, precision=PRECISE)  26.8 us
    reduce_sum x1, other arithmetic, local(): jnp.sum(grad_rows * padded[:, start_row:start_row + tok_rows], axis=(0, 1))  24.9 us
    convert_element_type x4, local copies, waits for them, and re-layouts, to_narrow(): signal.astype(jnp.bfloat16)  24.2 us
    unnamed x3, other arithmetic  23.6 us
  transfers between devices with their start and end apart: 8, of which 6 were waited for; matrix products, arithmetic and copies ran while one was open for 8% of the time, Pallas kernels for 0%

commit v1 on v0

v1 whole, which is shorter than its diff:
```python
import functools
import math

import jax
import jax.numpy as jnp
from jax import lax
from jax.experimental import pallas as pl
from jax.experimental.pallas import tpu as pltpu
from jax.sharding import PartitionSpec as P

GROUP = 16
LANES = 128
PER_BLOCK = LANES // GROUP
PRECISE = lax.Precision.HIGHEST
MESH = pl.DeviceIdType.MESH
ROWS = 16


def shifted(value, axis, steps):
    count = lax.axis_size(axis)
    leading, last = (max(0, -steps), min(count, count - steps))
    return lax.ppermute(value, axis, [(source, source + steps) for source in range(leading, last)])


def iota(shape, axis):
    return lax.broadcasted_iota(jnp.int32, shape, axis)


def halves(value):
    high = value.astype(jnp.bfloat16)
    return high, (value - high.astype(jnp.float32)).astype(jnp.bfloat16)


def dot(left, right, dims=((1,), (0,)), precision=None):
    return lax.dot_general(
        left, right, (dims, ((), ())), precision=precision, preferred_element_type=jnp.float32
    )


def flip_matrix(size):
    return (iota((size, size), 0) + iota((size, size), 1) == size - 1).astype(jnp.bfloat16)


def decay_table(rate_row, size):
    ages = (size - 1 - iota((size, LANES), 0)).astype(jnp.float32)
    table = jnp.exp(-(rate_row * ages))
    return table, ages * table


def to_row(value):
    rows = iota((LANES, LANES), 0)
    cols = iota((LANES, LANES), 1)
    same = (rows // GROUP == cols // GROUP).astype(jnp.float32)
    summed = dot(value, same, precision=PRECISE)
    pick = iota(value.shape, 0) == iota(value.shape, 1) % GROUP
    return jnp.sum(jnp.where(pick, summed, 0.0), axis=0, keepdims=True)


def to_wide(rate_row):
    rows = iota((LANES, LANES), 0)
    cols = iota((LANES, LANES), 1)
    same = (rows // GROUP == cols // GROUP).astype(jnp.float32)
    pick = iota((GROUP, LANES), 0) == iota((GROUP, LANES), 1) % GROUP
    return dot(jnp.where(pick, jnp.broadcast_to(rate_row, (GROUP, LANES)), 0.0), same, precision=PRECISE)


def delayed(value, halo):
    row = iota(value.shape, 0)
    one = jnp.where(row == 0, halo[1:2], pltpu.roll(value, 1, 0))
    two = jnp.where(row == 0, halo[0:1], jnp.where(row == 1, halo[1:2], pltpu.roll(value, 2, 0)))
    return one, two


def features_of(proj_ref, halo_ref, weight_ref, lanes):
    outs = []
    taps = []
    for part in range(3):
        now = proj_ref[part, :, lanes].astype(jnp.float32)
        halo = halo_ref[part, :, lanes].astype(jnp.float32)
        one, two = delayed(now, halo)
        weight = weight_ref[part, :, lanes]
        outs.append(now * weight[0:1] + one * weight[1:2] + two * weight[2:3])
        taps.append((now, one, two))
    return outs, taps


def gather_kernel(blocks, proj_ref, halo_ref, up_ref, weight_ref, rate_ref, x_ref, state_ref, slope_ref):
    size = proj_ref.shape[1]
    for block in range(blocks):
        lanes = pl.ds(block * LANES, LANES)
        (query, key, value), _ = features_of(proj_ref, halo_ref, weight_ref, lanes)
        gated = (key * value).astype(jnp.bfloat16)
        grad = (up_ref[:, lanes].astype(jnp.float32) * query).astype(jnp.bfloat16)
        turned = dot(flip_matrix(size), grad).astype(jnp.bfloat16)
        both = jnp.concatenate([gated, turned], axis=1)
        x_ref[block] = both
        table, slope = decay_table(rate_ref[block], size)
        keep = iota((LANES, 2 * LANES), 0) // GROUP == iota((LANES, 2 * LANES), 1) % LANES // GROUP
        for source, target in ((table, state_ref), (slope, slope_ref)):
            high, low = halves(source)
            full = dot(high, both, ((0,), (0,))) + dot(low, both, ((0,), (0,)))
            full = jnp.where(keep, full, 0.0)
            target[block] = jnp.sum(full.reshape(PER_BLOCK, GROUP, 2 * LANES), axis=0)


def inner_kernel(blocks, x_ref, rate_ref, gain_ref, y_ref, mode_ref):
    size = x_ref.shape[1]
    row = iota((size, LANES), 0)
    col = iota((size, LANES), 1)
    lane_group = col // GROUP
    wide_group = iota((size, 2 * LANES), 1) % LANES // GROUP
    small_keep = iota((PER_BLOCK, LANES), 0) == iota((PER_BLOCK, LANES), 1) // GROUP
    for block in range(blocks):
        both = x_ref[block]
        gated = both[:, :LANES]
        turned = both[:, LANES:]
        table, slope = decay_table(rate_ref[block], size)
        spread = jnp.where(small_keep, jnp.broadcast_to(gain_ref[block], (PER_BLOCK, LANES)), 0.0)
        taps = dot(spread, table, ((1,), (1,)), PRECISE)
        total = jnp.zeros((size, 2 * LANES), jnp.float32)
        sums = []
        for group in range(PER_BLOCK):
            line = jnp.broadcast_to(taps[group : group + 1], (size, LANES))
            band = pltpu.roll(line, 1, 1, stride=1, stride_axis=0)
            band = jnp.where(col <= row, band, 0.0).astype(jnp.bfloat16)
            total = jnp.where(wide_group == group, dot(band, both), total)
            chosen = jnp.where(lane_group == group, turned, jnp.zeros_like(turned))
            cross = dot(chosen, gated, ((1,), (1,)))
            cross = pltpu.roll(cross, 0, 1, stride=1, stride_axis=0)
            sums.append(jnp.sum(jnp.where(col >= row, cross, 0.0), axis=0, keepdims=True))
        y_ref[block] = total
        lags = jnp.concatenate(sums, axis=0)
        outs = []
        for source in (table, slope):
            spread = dot(lags, source, precision=PRECISE)
            outs.append(jnp.sum(jnp.where(small_keep, spread, 0.0), axis=0, keepdims=True))
        mode_ref[block] = jnp.concatenate(outs + [jnp.zeros((6, LANES), jnp.float32)], axis=0)


def scan_kernel(size, recv_ref, rate_ref, carry_ref, extra_ref):
    count = recv_ref.shape[0]
    for block in range(recv_ref.shape[1]):
        rate_row = rate_ref[block]
        decay = jnp.exp(-(to_wide(rate_row) * float(size)))
        held = jnp.zeros((GROUP, LANES), jnp.float32)
        aged = held
        plain = held
        weighted = held
        for step in range(count):
            begin = recv_ref[step, block, :, :LANES]
            other = recv_ref[step, block, :, LANES:]
            carry_ref[step, block, :, :LANES] = held
            plain = plain + other * held
            weighted = weighted + other * aged
            aged = decay * (aged + held)
            held = decay * held + begin
        held = jnp.zeros((GROUP, LANES), jnp.float32)
        for step in reversed(range(count)):
            carry_ref[step, block, :, LANES:] = held
            held = recv_ref[step, block, :, LANES:] + decay * held
        once = jnp.exp(-rate_row)
        extra_ref[block] = jnp.concatenate(
            [
                jnp.zeros((10, LANES), jnp.float32),
                once * to_row(plain),
                once * to_row(plain + float(size) * weighted),
                jnp.zeros((4, LANES), jnp.float32),
            ],
            axis=0,
        )


def outer_kernel(
    blocks, norm, proj_ref, halo_ref, up_ref, weight_ref, skip_ref, rate_ref, gain_ref, y_ref,
    carry_ref, slope_ref, mode_ref, mixed_ref, grad_ref, first_ref, last_ref, part_ref,
):
    size = proj_ref.shape[1]
    row = iota((size, LANES), 0)
    keep = iota((LANES, 2 * LANES), 0) // GROUP == iota((LANES, 2 * LANES), 1) % LANES // GROUP
    ages = (iota((size, LANES), 0) + 1).astype(jnp.float32)
    for block in range(blocks):
        lanes = pl.ds(block * LANES, LANES)
        (query, key, value), taps = features_of(proj_ref, halo_ref, weight_ref, lanes)
        gated = (key * value).astype(jnp.bfloat16).astype(jnp.float32)
        rate_row = rate_ref[block]
        coef = gain_ref[block] * jnp.exp(-(rate_row * ages))
        coef_high, coef_low = halves(coef)
        carry = carry_ref[block]
        spread = jnp.where(keep, jnp.concatenate([carry] * PER_BLOCK, axis=0), 0.0)
        high, low = halves(spread)
        whole = y_ref[block] + (dot(coef_high, high) + (dot(coef_high, low) + dot(coef_low, high)))
        narrow = whole.astype(jnp.bfloat16)
        convolved = narrow[:, :LANES].astype(jnp.float32)
        correlated = dot(flip_matrix(size), narrow[:, LANES:])
        upstream = up_ref[:, lanes].astype(jnp.float32)
        skip = skip_ref[:, lanes]
        grad_sum = upstream * query
        mixture = convolved + skip * gated
        mixed_ref[:, lanes] = (query * mixture).astype(jnp.bfloat16)
        grad_gate = correlated + skip * grad_sum
        lines = []
        for part, grads in enumerate((upstream * mixture, grad_gate * value, grad_gate * key)):
            weight = weight_ref[part, :, lanes]
            ahead = jnp.where(row < size - 1, pltpu.roll(grads, size - 1, 0), 0.0)
            further = jnp.where(row < size - 2, pltpu.roll(grads, size - 2, 0), 0.0)
            result = grads * weight[0:1] + ahead * weight[1:2] + further * weight[2:3]
            grad_ref[part, :, lanes] = result.astype(jnp.bfloat16)
            first_ref[part, :, lanes] = grads[:8]
            last_ref[part, :, lanes] = result[size - 8 :]
            for tap in taps[part]:
                lines.append(jnp.sum(grads * tap, axis=0, keepdims=True) * norm)
        lines.append(jnp.sum(grad_sum * gated, axis=0, keepdims=True) * norm)
        slopes = slope_ref[block]
        between = slopes[:, LANES:] * carry[:, :LANES] + slopes[:, :LANES] * carry[:, LANES:]
        modes = mode_ref[block]
        lines.append(modes[0:1])
        lines.append(modes[1:2] + jnp.exp(-rate_row) * to_row(between))
        lines.append(jnp.zeros((4, LANES), jnp.float32))
        part_ref[block] = jnp.concatenate(lines, axis=0)


def mend_kernel(grad_ref, last_ref, after_ref, weight_ref, out_ref):
    for part in range(3):
        tile = grad_ref[part]
        last = last_ref[part]
        after = after_ref[part]
        weight = weight_ref[part]
        late = last[6:7] + after[0:1] * weight[2:3]
        final = last[7:8] + after[0:1] * weight[1:2] + after[1:2] * weight[2:3]
        row = iota(tile.shape, 0)
        wide = jnp.where(row == 14, late, jnp.where(row == 15, final, tile.astype(jnp.float32)))
        out_ref[part] = wide.astype(jnp.bfloat16)


def reduce_kernel(
    counts, part_ref, extra_ref, out_ref, near_ref, sum_ref, far_ref, done_ref,
    send_one, recv_one, send_two, recv_two, send_three, recv_three,
):
    dp_count, ctx_count, tp_count = counts
    dp, ctx, tp = lax.axis_index("dp"), lax.axis_index("ctx"), lax.axis_index("tp")
    others = [(a, b) for b in range(tp_count) for a in range(dp_count) if (a, b) != (0, 0)]

    def ring(step):
        return {"ctx": lax.rem(ctx + step, ctx_count)}

    def cross(pair):
        return {"dp": lax.rem(dp + pair[0], dp_count), "tp": lax.rem(tp + pair[1], tp_count)}

    barrier = pltpu.get_barrier_semaphore()
    for step in range(1, ctx_count):
        pl.semaphore_signal(barrier, inc=1, device_id=ring(step), device_id_type=MESH)
    for pair in others:
        pl.semaphore_signal(barrier, inc=1, device_id=cross(pair), device_id_type=MESH)
    pl.semaphore_wait(barrier, ctx_count - 1 + len(others))

    first = []
    for step in range(1, ctx_count):
        first.append(
            pltpu.make_async_remote_copy(
                part_ref.at[lax.rem(ctx + step, ctx_count)], near_ref.at[step],
                send_one.at[step], recv_one.at[step], device_id=ring(step), device_id_type=MESH,
            )
        )
        first[-1].start()
    total = part_ref[ctx] + extra_ref[...]
    for step in range(1, ctx_count):
        first[step - 1].wait_recv()
        total = total + near_ref[step]
    sum_ref[...] = total

    second = []
    for index, pair in enumerate(others):
        second.append(
            pltpu.make_async_remote_copy(
                sum_ref, far_ref.at[index], send_two.at[index], recv_two.at[index],
                device_id=cross(pair), device_id_type=MESH,
            )
        )
        second[-1].start()
    foreign = jnp.zeros_like(total)
    for index, pair in enumerate(others):
        second[index].wait_recv()
        if pair[1] == 0:
            total = total + far_ref[index]
        else:
            foreign = foreign + far_ref[index]
    moved = pltpu.roll(foreign, 2, 1)
    row = iota(total.shape, 1)
    total = jnp.where((row == 12) | (row == 13), moved, total)
    done_ref[...] = total

    third = []
    for step in range(1, ctx_count):
        third.append(
            pltpu.make_async_remote_copy(
                done_ref, out_ref.at[ctx], send_three.at[step], recv_three.at[step],
                device_id=ring(step), device_id_type=MESH,
            )
        )
        third[-1].start()
    out_ref[ctx] = total
    for copy in third:
        copy.wait_recv()
    for copy in first + second + third:
        copy.wait_send()


def local(projected, upstream, short_weight, skip_gain, residues, rates):
    size = projected.shape[1]
    width = projected.shape[3]
    dp_count, ctx_count, tp_count = (lax.axis_size(name) for name in ("dp", "ctx", "tp"))
    block_count = width // LANES
    own_blocks = block_count // ctx_count
    group_count = width // GROUP
    blocks = math.gcd(block_count, 4)
    norm = 1.0 / math.sqrt(dp_count * ctx_count * size)

    proj = projected[0].transpose(1, 0, 2)
    up = upstream[0]
    before = shifted(proj[:, size - 2 :], "ctx", 1)
    tp = lax.axis_index("tp")
    ctx = lax.axis_index("ctx")
    my_rates = lax.dynamic_slice_in_dim(rates, tp * group_count, group_count, 0)
    my_residues = lax.dynamic_slice_in_dim(residues, tp * group_count, group_count, 0)
    rate_rows = my_rates.reshape(block_count, 1, LANES)
    gain_rows = (my_residues * jnp.sqrt(my_rates)).reshape(block_count, 1, LANES)
    own_rates = lax.dynamic_slice_in_dim(rate_rows, ctx * own_blocks, own_blocks, 0)
    skip_row = skip_gain.reshape(1, width)

    grid = (block_count // blocks,)
    step_width = blocks * LANES
    wide3 = pl.BlockSpec((3, size, step_width), lambda i: (0, 0, i))
    halo3 = pl.BlockSpec((3, 2, step_width), lambda i: (0, 0, i))
    tile3 = pl.BlockSpec((3, 8, step_width), lambda i: (0, 0, i))
    taps3 = pl.BlockSpec((3, 3, step_width), lambda i: (0, 0, i))
    flat = pl.BlockSpec((size, step_width), lambda i: (0, i))
    line = pl.BlockSpec((1, step_width), lambda i: (0, i))

    def stacked(rows, cols):
        return pl.BlockSpec((blocks, rows, cols), lambda i: (i, 0, 0))

    def array(*shape, kind=jnp.float32):
        return jax.ShapeDtypeStruct(shape, kind)

    row_spec = stacked(1, LANES)
    params = pltpu.CompilerParams(dimension_semantics=("arbitrary",))

    x, states, slopes = pl.pallas_call(
        functools.partial(gather_kernel, blocks),
        grid=grid,
        in_specs=[wide3, halo3, flat, taps3, row_spec],
        out_specs=[stacked(size, 2 * LANES), stacked(GROUP, 2 * LANES), stacked(GROUP, 2 * LANES)],
        out_shape=[
            array(block_count, size, 2 * LANES, kind=jnp.bfloat16),
            array(block_count, GROUP, 2 * LANES),
            array(block_count, GROUP, 2 * LANES),
        ],
        compiler_params=params,
        name="states",
    )(proj, before, up, short_weight, rate_rows)

    received = lax.all_to_all(
        states.reshape(ctx_count, own_blocks, GROUP, 2 * LANES), "ctx", 0, 0, tiled=True
    )

    y, modes = pl.pallas_call(
        functools.partial(inner_kernel, blocks),
        grid=grid,
        in_specs=[stacked(size, 2 * LANES), row_spec, row_spec],
        out_specs=[stacked(size, 2 * LANES), stacked(8, LANES)],
        out_shape=[array(block_count, size, 2 * LANES), array(block_count, 8, LANES)],
        compiler_params=params,
        cost_estimate=pl.CostEstimate(
            flops=4 * block_count * 8 * size * size * LANES * 3,
            bytes_accessed=block_count * size * 256 * 6,
            transcendentals=block_count * size * LANES,
        ),
        name="inner",
    )(x, rate_rows, gain_rows)

    carry, extra = pl.pallas_call(
        functools.partial(scan_kernel, size),
        out_shape=[
            array(ctx_count, own_blocks, GROUP, 2 * LANES),
            array(own_blocks, ROWS, LANES),
        ],
        name="scan",
    )(received, own_rates)
    carry = lax.all_to_all(carry, "ctx", 0, 0, tiled=True).reshape(block_count, GROUP, 2 * LANES)

    mixed, grad, first, last, part = pl.pallas_call(
        functools.partial(outer_kernel, blocks, norm),
        grid=grid,
        in_specs=[
            wide3, halo3, flat, taps3, line, row_spec, row_spec, stacked(size, 2 * LANES),
            stacked(GROUP, 2 * LANES), stacked(GROUP, 2 * LANES), stacked(8, LANES),
        ],
        out_specs=[flat, wide3, tile3, tile3, stacked(ROWS, LANES)],
        out_shape=[
            array(size, width, kind=jnp.bfloat16),
            array(3, size, width, kind=jnp.bfloat16),
            array(3, 8, width),
            array(3, 8, width),
            array(block_count, ROWS, LANES),
        ],
        compiler_params=params,
        name="outer",
    )(proj, before, up, short_weight, skip_row, rate_rows, gain_rows, y, carry, slopes, modes)

    after = shifted(first[:, :2], "ctx", -1)

    others = dp_count * tp_count - 1
    summed = pl.pallas_call(
        functools.partial(reduce_kernel, (dp_count, ctx_count, tp_count)),
        in_specs=[pl.BlockSpec(memory_space=pltpu.VMEM)] * 2,
        out_specs=pl.BlockSpec(memory_space=pltpu.VMEM),
        out_shape=array(ctx_count, own_blocks, ROWS, LANES),
        scratch_shapes=[
            pltpu.VMEM((ctx_count, own_blocks, ROWS, LANES), jnp.float32),
            pltpu.VMEM((own_blocks, ROWS, LANES), jnp.float32),
            pltpu.VMEM((max(others, 1), own_blocks, ROWS, LANES), jnp.float32),
            pltpu.VMEM((own_blocks, ROWS, LANES), jnp.float32),
            pltpu.SemaphoreType.DMA((ctx_count,)),
            pltpu.SemaphoreType.DMA((ctx_count,)),
            pltpu.SemaphoreType.DMA((max(others, 1),)),
            pltpu.SemaphoreType.DMA((max(others, 1),)),
            pltpu.SemaphoreType.DMA((ctx_count,)),
            pltpu.SemaphoreType.DMA((ctx_count,)),
        ],
        compiler_params=pltpu.CompilerParams(collective_id=0, has_side_effects=True),
        name="reduce",
    )(part.reshape(ctx_count, own_blocks, ROWS, LANES), extra)

    mend_width = math.gcd(width, 1024)
    tail = pl.BlockSpec((3, 16, mend_width), lambda i: (0, size // 16 - 1, i))
    grad = pl.pallas_call(
        mend_kernel,
        grid=(width // mend_width,),
        in_specs=[
            tail,
            pl.BlockSpec((3, 8, mend_width), lambda i: (0, 0, i)),
            pl.BlockSpec((3, 2, mend_width), lambda i: (0, 0, i)),
            pl.BlockSpec((3, 3, mend_width), lambda i: (0, 0, i)),
        ],
        out_specs=tail,
        out_shape=array(3, size, width, kind=jnp.bfloat16),
        input_output_aliases={0: 0},
        compiler_params=params,
        name="mend",
    )(grad, last, after, short_weight)

    flat_sums = summed.reshape(block_count, ROWS, LANES)
    grad_short = flat_sums[:, :9].transpose(1, 0, 2).reshape(3, 3, width)
    grad_skip = flat_sums[:, 9].reshape(width)

    def both_halves(index):
        mine = flat_sums[:, 10 + index].reshape(1, group_count, GROUP)
        if tp_count == 1:
            return mine.reshape(group_count, GROUP)
        other = flat_sums[:, 12 + index].reshape(1, group_count, GROUP)
        low = jnp.where(tp == 0, mine, other)
        high = jnp.where(tp == 0, other, mine)
        return jnp.concatenate([low, high], axis=0).reshape(2 * group_count, GROUP)

    sum_plain = both_halves(0)
    sum_weighted = both_halves(1)
    root = jnp.sqrt(rates)
    grad_residues = root * sum_plain * norm
    grad_log_rates = residues * (0.5 * root * sum_plain - rates * root * sum_weighted) * norm
    return (
        mixed[None],
        grad.transpose(1, 0, 2)[None],
        grad_short,
        grad_skip,
        grad_residues,
        grad_log_rates,
    )


def solution(mesh):
    in_specs = (
        P("dp", "ctx", None, "tp"),
        P("dp", "ctx", "tp"),
        P(None, None, "tp"),
        P("tp"),
        P(),
        P(),
    )
    out_specs = (
        P("dp", "ctx", "tp"),
        P("dp", "ctx", None, "tp"),
        P(None, None, "tp"),
        P("tp"),
        P(),
        P(),
    )
    return jax.shard_map(local, mesh=mesh, in_specs=in_specs, out_specs=out_specs, check_vma=False)
```

time: 1060 us -> 133 us (0.13)
  waiting for transfers between devices: 381 us -> 9.11 us
  blocking collectives: 272 us -> 0 us
  other arithmetic: 137 us -> 1.47 us
  local copies, waits for them, and re-layouts: 144 us -> 12.1 us
  Pallas kernels: 0 us -> 91.1 us
  matrix products: 78.9 us -> 0 us
  between operations: 15 us -> 0.77 us
    psum x2 -> x0, waiting for transfers between devices: 359 us -> none  [the longest x1 216 us: local(): grad_short, grad_skip = lax.psum((short_local, skip_local), ('dp', 'ctx'))]
    psum x1 -> x0, blocking collectives: 272 us -> none  [local(): grad_short, grad_skip = lax.psum((short_local, skip_local), ('dp', 'ctx'))]
    pallas_call x0 -> x6, Pallas kernels: none -> 91.1 us  [the longest x1 36.6 us: local(): pl.pallas_call(functools.partial(inner_kernel, blocks), grid=grid, in_spe...]
    dot_general x14 -> x0, matrix products: 78.9 us -> none  [the longest x3 26.8 us: spectrum(): return jnp.einsum('bzkpc,zpyj->bykjc', turned, table_two, precision=PRECISE)]
    add x4 -> x0, other arithmetic: 32.1 us -> none  [the longest x1 9.86 us: local(): real_g * real_d + imag_g * imag_d]
    reduce_sum x3 -> x0, other arithmetic: 31.2 us -> none  [the longest x1 24.9 us: local(): jnp.sum(grad_rows * padded[:, start_row:start_row + tok_rows], axis=(0, 1))]
    unnamed x93 -> x12, local copies, waits for them, and re-layouts: 32.5 us -> 2.85 us
    convert_element_type x7 -> x0, local copies, waits for them, and re-layouts: 29.1 us -> none  [the longest x4 24.2 us: to_narrow(): signal.astype(jnp.bfloat16)]
  transfers between devices with their start and end apart: 8 -> 4, of which waited for: 6 -> 2; matrix products, arithmetic and copies ran while one was open for 8% -> 4% of each run, Pallas kernels for 0% -> 28%
where the time goes in v1:
time: 133 us; the launch traced here: 132 us
  Pallas kernels  91.1 us (68%)
  starting transfers between devices  17.7 us (13%)
  local copies, waits for them, and re-layouts  12.1 us (9%)
  waiting for transfers between devices  9.11 us (7%)
  other arithmetic  1.47 us (1%)
    pallas_call x1, Pallas kernels, local(): pl.pallas_call(functools.partial(inner_kernel, blocks), grid=grid, in_spe...  36.6 us
    pallas_call x1, Pallas kernels, local(): pl.pallas_call(functools.partial(reduce_kernel, (dp_count, ctx_count, tp_...  25.1 us
    pallas_call x1, Pallas kernels, local(): pl.pallas_call(functools.partial(outer_kernel, blocks, norm), grid=grid,...  13.3 us
    pallas_call x1, Pallas kernels, local(): pl.pallas_call(functools.partial(gather_kernel, blocks), grid=grid, in_sp...  10.4 us
    all_to_all x1, waiting for transfers between devices, local(): lax.all_to_all(states.reshape(ctx_count, own_blocks, GROUP, 2 * LANES), '...  7.61 us
    ppermute x2, starting transfers between devices, shifted(): lax.ppermute(value, axis, [(source, source + steps) for source in range(l...  6.8 us
    all_to_all x1, starting transfers between devices, local(): lax.all_to_all(states.reshape(ctx_count, own_blocks, GROUP, 2 * LANES), '...  6.23 us
    all_to_all x1, starting transfers between devices, local(): lax.all_to_all(carry, 'ctx', 0, 0, tiled=True)  4.62 us
  transfers between devices with their start and end apart: 4, of which 2 were waited for; matrix products, arithmetic and copies ran while one was open for 4% of the time, Pallas kernels for 28%

profile of v1, /device:TPU:1, one launch (start us, length us, event | category | flops | bytes accessed | tf_op | source)
XLA Modules:
  0.0 132.2 jit_solution(11336812046317962025)
XLA Ops:
  0.6 1.0 slice.32
  1.6 4.5 %collective-permute-start = (bf16[3,2,4096]{2,1,0:T(2,128)(2,1)S(1)}, bf16[3,2,4096]{2,1,0:T(2,128)(2,1)S(1)}, u32[]{:S(2)}, u32[]{:S(2)}) collective-permute-start(bf16[3,2,4096]{2,1,0:T(2,128)(2,1)S(1)} %slice.32), channel_id=1, source_target_pairs={{0,2},{2,4},{4,6},{6,8},{8,10},{10,12},{12,14},{14,16},{16,18},{18... | collective-permute-start | bytes 147464 | tf_op jit(solution)/shard_map/ppermute | solution.py:22
  6.1 0.7 sqrt_multiply_fusion.3
  6.9 0.1 copy.72
  7.0 0.7 reshape.131
  7.7 0.0 collective-permute-done.halo_ref
  7.7 0.0 copy-start.2
  7.7 0.6 copy-done.2
  8.3 10.4 %states.1 = (bf16[32,128,256]{2,1,0:T(8,128)(2,1)}, f32[32,16,256]{2,1,0:T(8,128)}, f32[32,16,256]{2,1,0:T(8,128)}) custom-call(bf16[3,128,4096]{2,1,0:T(8,128)(2,1)} %bitcast.33, bf16[3,2,4096]{2,1,0:T(2,128)(2,1)} %copy-done.2, bf16[128,4096]{1,0:T(8,128)(2,1)} %bitcast.35, f32[3,3,4096]{2,1,0:T(4,128)} %weight_ref.5, f32[32,1,128]{2,1,0:T(1,128)} %bitcast.45), custom_call_target="tpu_custom_call" | custom-call | tf_op jit(solution)/shard_map/states/pallas_call | solution.py:348
  18.7 6.2 %all-to-all-start = ((f32[16,2,16,256]{3,2,1,0:T(8,128)}), f32[16,2,16,256]{3,2,1,0:T(8,128)S(1)}, u32[]{:S(2)}, u32[]{:S(2)}) async-start(f32[16,2,16,256]{3,2,1,0:T(8,128)} %bitcast.43), calls=%async_computation | async-start | bytes 1048576 | tf_op jit(solution)/shard_map/all_to_all | solution.py:362
  24.9 0.1 copy.73
  25.0 0.7 reshape.132
  25.7 1.2 constant_dynamic-slice_fusion.rate_ref
  27.0 7.6 %all-to-all-done.recv_ref = f32[16,2,16,256]{3,2,1,0:T(8,128)S(1)} async-done(((f32[16,2,16,256]{3,2,1,0:T(8,128)}), f32[16,2,16,256]{3,2,1,0:T(8,128)S(1)}, u32[]{:S(2)}, u32[]{:S(2)}) %all-to-all-start) | async-done | bytes 524320 | tf_op jit(solution)/shard_map/all_to_all | solution.py:362
  34.6 0.0 copy-start.1
  34.6 0.8 copy-done.1
  35.4 2.5 %scan.1 = (f32[16,2,16,256]{3,2,1,0:T(8,128)}, f32[2,16,128]{2,1,0:T(8,128)}) custom-call(f32[16,2,16,256]{3,2,1,0:T(8,128)} %copy-done.1, f32[2,1,128]{2,1,0:T(1,128)} %constant_dynamic-slice_fusion.rate_ref), custom_call_target="tpu_custom_call" | custom-call | tf_op jit(solution)/shard_map/scan/pallas_call | solution.py:381
  37.9 4.6 %all-to-all-start.1 = ((f32[16,2,16,256]{3,2,1,0:T(8,128)}), f32[16,2,16,256]{3,2,1,0:T(8,128)S(1)}, u32[]{:S(2)}, u32[]{:S(2)}) async-start(f32[16,2,16,256]{3,2,1,0:T(8,128)} %get-tuple-element.21), calls=%async_computation.1 | async-start | bytes 1048576 | tf_op jit(solution)/shard_map/all_to_all | solution.py:389
  42.5 36.6 %inner.1 = (f32[32,128,256]{2,1,0:T(8,128)}, f32[32,8,128]{2,1,0:T(8,128)}) custom-call(bf16[32,128,256]{2,1,0:T(8,128)(2,1)} %get-tuple-element.18.x_ref, f32[32,1,128]{2,1,0:T(1,128)} %bitcast.47, f32[32,1,128]{2,1,0:T(1,128)} %bitcast.49), custom_call_target="tpu_custom_call" | custom-call | flops 6442450944 | bytes 6291456 | tf_op jit(solution)/shard_map/inner/pallas_call | solution.py:366
  79.1 0.0 all-to-all-done.1
  79.1 0.0 copy-start
  79.1 0.8 copy-done
  79.9 13.3 %outer.1 = (bf16[128,4096]{1,0:T(8,128)(2,1)}, bf16[3,128,4096]{2,1,0:T(8,128)(2,1)}, f32[3,8,4096]{2,1,0:T(8,128)}, f32[3,8,4096]{2,1,0:T(8,128)}, f32[32,16,128]{2,1,0:T(8,128)}) custom-call(bf16[3,128,4096]{2,1,0:T(8,128)(2,1)} %bitcast.34, bf16[3,2,4096]{2,1,0:T(2,128)(2,1)} %copy-done.2, bf16[128,4096]{1,0:T(8,128)(2,1)} %bitcast.36, ...), custom_call_target="tpu_custom_call" | custom-call | tf_op jit(solution)/shard_map/outer/pallas_call | solution.py:391
  93.2 0.0 copy-start.4
  93.2 0.0 copy-start.5
  93.2 25.1 %reduce.1 = f32[16,2,16,128]{3,2,1,0:T(8,128)} custom-call(f32[16,2,16,128]{3,2,1,0:T(8,128)} %bitcast.44, f32[2,16,128]{2,1,0:T(8,128)} %get-tuple-element.29.extra_ref), custom_call_target="tpu_custom_call" | custom-call | tf_op jit(solution)/shard_map/reduce/pallas_call | solution.py:413
  118.3 2.0 %fusion.6 = (f32[32,1,128]{2,1,0:T(1,128)S(1)}, f32[32,1,128]{2,1,0:T(1,128)S(1)}, f32[32,1,128]{2,1,0:T(1,128)S(1)}, f32[32,1,128]{2,1,0:T(1,128)S(1)}, f32[32,1,128]{2,1,0:T(1,128)}) fusion(f32[32,16,128]{2,1,0:T(8,128)} %bitcast.39), kind=kLoop, calls=%fused_computation.19 | loop fusion | bytes 163840 | tf_op jit(solution)/shard_map/slice | solution.py:457
  120.3 1.0 slice_bitcast_fusion
  121.3 1.0 slice.25
  122.3 2.3 %collective-permute-start.1 = (f32[3,2,4096]{2,1,0:T(2,128)S(1)}, f32[3,2,4096]{2,1,0:T(2,128)S(1)}, u32[]{:S(2)}, u32[]{:S(2)}) collective-permute-start(f32[3,2,4096]{2,1,0:T(2,128)S(1)} %slice.25), channel_id=1, source_target_pairs={{2,0},{4,2},{6,4},{8,6},{10,8},{12,10},{14,12},{16,14},{18,16},{20... | collective-permute-start | bytes 294920 | tf_op jit(solution)/shard_map/ppermute | solution.py:22
  124.7 0.1 select_n.79
  124.8 0.1 select_n.81
  124.9 0.1 copy.88
  125.0 0.1 select_n.77
  125.1 0.1 select_n.75
  125.2 0.1 copy.87
  125.3 0.0 copy-done.4
  125.3 0.0 copy-done.5
  125.3 0.7 fusion.4
  126.0 0.7 reshape.137
  126.8 1.5 %collective-permute-done.1.after_ref = f32[3,2,4096]{2,1,0:T(2,128)S(1)} collective-permute-done((f32[3,2,4096]{2,1,0:T(2,128)S(1)}, f32[3,2,4096]{2,1,0:T(2,128)S(1)}, u32[]{:S(2)}, u32[]{:S(2)}) %collective-permute-start.1) | collective-permute-done | bytes 98336 | tf_op jit(solution)/shard_map/ppermute | solution.py:22
  128.3 0.0 copy-start.3
  128.3 0.6 copy-done.3
  128.9 3.3 %mend.1 = bf16[3,128,4096]{2,1,0:T(8,128)(2,1)} custom-call(bf16[3,128,4096]{2,1,0:T(8,128)(2,1)} %get-tuple-element.25.grad_ref, f32[3,8,4096]{2,1,0:T(8,128)} %get-tuple-element.26.last_ref, f32[3,2,4096]{2,1,0:T(2,128)} %copy-done.3, f32[3,3,4096]{2,1,0:T(4,128)} %weight_ref.5), custom_call_target="tpu_custom_call", output_to_operand_aliasing={{}: (0, {})} | custom-call | tf_op jit(solution)/shard_map/mend/pallas_call | solution.py:436
  (4 shorter events, 0.1 us)
Async XLA Ops:
  1.6 6.1 %collective-permute-start = (bf16[3,2,4096]{2,1,0:T(2,128)(2,1)S(1)}, bf16[3,2,4096]{2,1,0:T(2,128)(2,1)S(1)}, u32[]{:S(2)}, u32[]{:S(2)}) collective-permute-start(bf16[3,2,4096]{2,1,0:T(2,128)(2,1)S(1)} %slice.32), channel_id=1, source_target_pairs={{0,2},{2,4},{4,6},{6,8},{8,10},{10,12},{12,14},{14,16},{16,18},{18... | collective-permute-start | bytes 147464 | tf_op jit(solution)/shard_map/ppermute | solution.py:22
  7.7 0.6 copy-start.2
  18.7 15.9 %all-to-all-start = ((f32[16,2,16,256]{3,2,1,0:T(8,128)}), f32[16,2,16,256]{3,2,1,0:T(8,128)S(1)}, u32[]{:S(2)}, u32[]{:S(2)}) async-start(f32[16,2,16,256]{3,2,1,0:T(8,128)} %bitcast.43), calls=%async_computation | async-start | bytes 1048576 | tf_op jit(solution)/shard_map/all_to_all | solution.py:362
  34.6 0.8 copy-start.1
  37.9 41.2 %all-to-all-start.1 = ((f32[16,2,16,256]{3,2,1,0:T(8,128)}), f32[16,2,16,256]{3,2,1,0:T(8,128)S(1)}, u32[]{:S(2)}, u32[]{:S(2)}) async-start(f32[16,2,16,256]{3,2,1,0:T(8,128)} %get-tuple-element.21), calls=%async_computation.1 | async-start | bytes 1048576 | tf_op jit(solution)/shard_map/all_to_all | solution.py:389
  79.1 0.8 copy-start
  93.2 32.1 %copy-start.4 = (f32[512,16]{0,1:T(8,128)S(1)}, f32[512,16]{0,1:T(8,128)}, u32[]{:S(2)}) copy-start(f32[512,16]{0,1:T(8,128)} %param.10) | copy-start | bytes 98308
  93.2 32.1 %copy-start.5 = (f32[512,16]{0,1:T(8,128)S(1)}, f32[512,16]{0,1:T(8,128)}, u32[]{:S(2)}) copy-start(f32[512,16]{0,1:T(8,128)} %param.11) | copy-start | bytes 98308
  122.3 5.9 %collective-permute-start.1 = (f32[3,2,4096]{2,1,0:T(2,128)S(1)}, f32[3,2,4096]{2,1,0:T(2,128)S(1)}, u32[]{:S(2)}, u32[]{:S(2)}) collective-permute-start(f32[3,2,4096]{2,1,0:T(2,128)S(1)} %slice.25), channel_id=1, source_target_pairs={{2,0},{4,2},{6,4},{8,6},{10,8},{12,10},{14,12},{16,14},{18,16},{20... | collective-permute-start | bytes 294920 | tf_op jit(solution)/shard_map/ppermute | solution.py:22
  128.3 0.6 copy-start.3

commit v2 on v1

--- a/solution.py
+++ b/solution.py
@@ -14,6 +14,7 @@
 PRECISE = lax.Precision.HIGHEST
 MESH = pl.DeviceIdType.MESH
 ROWS = 16
+SUB = 32
 
 
 def shifted(value, axis, steps):
@@ -103,42 +104,95 @@
             target[block] = jnp.sum(full.reshape(PER_BLOCK, GROUP, 2 * LANES), axis=0)
 
 
-def inner_kernel(blocks, x_ref, rate_ref, gain_ref, y_ref, mode_ref):
+def inner_blocks(base, blocks, x_ref, rate_ref, gain_ref, y_ref, mode_ref):
     size = x_ref.shape[1]
-    row = iota((size, LANES), 0)
-    col = iota((size, LANES), 1)
-    lane_group = col // GROUP
-    wide_group = iota((size, 2 * LANES), 1) % LANES // GROUP
+    runs = size // SUB
     small_keep = iota((PER_BLOCK, LANES), 0) == iota((PER_BLOCK, LANES), 1) // GROUP
-    for block in range(blocks):
-        both = x_ref[block]
-        gated = both[:, :LANES]
-        turned = both[:, LANES:]
-        table, slope = decay_table(rate_ref[block], size)
-        spread = jnp.where(small_keep, jnp.broadcast_to(gain_ref[block], (PER_BLOCK, LANES)), 0.0)
-        taps = dot(spread, table, ((1,), (1,)), PRECISE)
-        total = jnp.zeros((size, 2 * LANES), jnp.float32)
-        sums = []
+    lag_lane = iota((PER_BLOCK, LANES), 1)
+    lag_seat = iota((PER_BLOCK, LANES), 0) % runs
+    keep = (
+        iota((PER_BLOCK * SUB, 2 * LANES), 0) // SUB
+        == iota((PER_BLOCK * SUB, 2 * LANES), 1) % LANES // GROUP
+    )
+    causal = iota((SUB, size), 1) >= iota((SUB, size), 0)
+    parity = iota((SUB, LANES), 1) // SUB % 2
+    steps = iota((size, LANES), 0).astype(jnp.float32)
+    every = range(blocks)
+    tables = [decay_table(rate_ref[base + block], size) for block in every]
+    taps = []
+    for block in every:
+        forward = jnp.exp(-(rate_ref[base + block] * steps))
+        spread = jnp.where(small_keep, jnp.broadcast_to(gain_ref[base + block], (PER_BLOCK, LANES)), 0.0)
+        taps.append(dot(spread, forward, ((1,), (1,)), PRECISE))
+    chosen = []
+    for block in every:
+        picks = []
+        for run in range(runs):
+            tiled = jnp.concatenate([x_ref[base + block, run * SUB : (run + 1) * SUB]] * PER_BLOCK, axis=0)
+            picks.append(jnp.where(keep, tiled, jnp.zeros_like(tiled)))
+        chosen.append(picks)
+
+    def stepped(value):
+        parts = [value]
+        for run in range(1, runs):
+            blank = jnp.zeros((run * SUB, value.shape[1]), value.dtype)
+            parts.append(jnp.concatenate([blank, value[: size - run * SUB]], axis=0))
+        return jnp.concatenate(parts, axis=1)
+
+    crosses = [
+        dot(
+            stepped(x_ref[base + block, :, LANES:]),
+            jnp.concatenate([value[:, :LANES] for value in chosen[block]], axis=1),
+            ((1,), (1,)),
+        )
+        for block in every
+    ]
+    lefts = []
+    for block in every:
+        bands = []
         for group in range(PER_BLOCK):
-            line = jnp.broadcast_to(taps[group : group + 1], (size, LANES))
-            band = pltpu.roll(line, 1, 1, stride=1, stride_axis=0)
-            band = jnp.where(col <= row, band, 0.0).astype(jnp.bfloat16)
-            total = jnp.where(wide_group == group, dot(band, both), total)
-            chosen = jnp.where(lane_group == group, turned, jnp.zeros_like(turned))
-            cross = dot(chosen, gated, ((1,), (1,)))
-            cross = pltpu.roll(cross, 0, 1, stride=1, stride_axis=0)
-            sums.append(jnp.sum(jnp.where(col >= row, cross, 0.0), axis=0, keepdims=True))
-        y_ref[block] = total
-        lags = jnp.concatenate(sums, axis=0)
-        outs = []
-        for source in (table, slope):
-            spread = dot(lags, source, precision=PRECISE)
-            outs.append(jnp.sum(jnp.where(small_keep, spread, 0.0), axis=0, keepdims=True))
-        mode_ref[block] = jnp.concatenate(outs + [jnp.zeros((6, LANES), jnp.float32)], axis=0)
-
-
-def scan_kernel(size, recv_ref, rate_ref, carry_ref, extra_ref):
-    count = recv_ref.shape[0]
+            line = jnp.broadcast_to(taps[block][group : group + 1], (SUB, size))
+            line = pltpu.roll(line, 0, 1, stride=1, stride_axis=0)
+            bands.append(jnp.where(causal, line, 0.0))
+        lefts.append(jnp.concatenate(bands, axis=0).T.astype(jnp.bfloat16))
+    for block in every:
+        y_ref[base + block] = dot(stepped(lefts[block]), jnp.concatenate(chosen[block], axis=0))
+    lags = []
+    for block in every:
+        packed = []
+        for run in range(runs):
+            lines = []
+            for tile in range(2):
+                part = crosses[block][run * SUB : (run + 1) * SUB, tile * LANES : (tile + 1) * LANES]
+                two = []
+                for odd in range(2):
+                    moved = jnp.where(parity == odd, part, 0.0)
+                    moved = pltpu.roll(moved, 0, 1, stride=1, stride_axis=0)
+                    two.append(jnp.sum(moved, axis=0, keepdims=True))
+                lines += [two[0], two[1], two[0], two[1]]
+            packed.append(jnp.concatenate(lines, axis=0))
+        total = jnp.zeros((PER_BLOCK, LANES), jnp.float32)
+        for turn in range(runs):
+            lag_run = (lag_seat + turn) % runs
+            lines = packed[0]
+            for run in range(1, runs):
+                lines = jnp.where(lag_run == run, packed[run], lines)
+            if turn:
+                lines = pltpu.roll(lines, turn * SUB, 1)
+            begin = lag_run * SUB
+            inside = (lag_lane >= begin) & (lag_lane < begin + 2 * SUB - 1)
+            total = total + jnp.where(inside, lines, 0.0)
+        lags.append(total)
+    spreads = [[dot(lags[block], source, precision=PRECISE) for source in tables[block]] for block in every]
+    for block in every:
+        outs = [
+            jnp.sum(jnp.where(small_keep, spread, 0.0), axis=0, keepdims=True) for spread in spreads[block]
+        ]
+        mode_ref[base + block] = jnp.concatenate(outs + [jnp.zeros((6, LANES), jnp.float32)], axis=0)
+
+
+def scan_states(size, ctx, count, recv_ref, rate_ref, carry_ref, extra_ref):
+    slots = [lax.rem(ctx - step + count, count) for step in range(count)]
     for block in range(recv_ref.shape[1]):
         rate_row = rate_ref[block]
         decay = jnp.exp(-(to_wide(rate_row) * float(size)))
@@ -147,8 +201,8 @@
         plain = held
         weighted = held
         for step in range(count):
-            begin = recv_ref[step, block, :, :LANES]
-            other = recv_ref[step, block, :, LANES:]
+            begin = recv_ref[slots[step], block, :, :LANES]
+            other = recv_ref[slots[step], block, :, LANES:]
             carry_ref[step, block, :, :LANES] = held
             plain = plain + other * held
             weighted = weighted + other * aged
@@ -157,7 +211,7 @@
         held = jnp.zeros((GROUP, LANES), jnp.float32)
         for step in reversed(range(count)):
             carry_ref[step, block, :, LANES:] = held
-            held = recv_ref[step, block, :, LANES:] + decay * held
+            held = recv_ref[slots[step], block, :, LANES:] + decay * held
         once = jnp.exp(-rate_row)
         extra_ref[block] = jnp.concatenate(
             [
@@ -168,6 +222,56 @@
             ],
             axis=0,
         )
+
+
+def exchange_kernel(
+    ctx_count, blocks, early, state_ref, x_ref, rate_ref, gain_ref, own_ref, y_ref, mode_ref, carry_ref,
+    extra_ref, near_ref, back_ref, send_one, recv_one, send_two, recv_two,
+):
+    ctx = lax.axis_index("ctx")
+    size = x_ref.shape[1]
+    rounds = x_ref.shape[0] // blocks
+
+    def peer(step):
+        return lax.rem(ctx + step, ctx_count)
+
+    def work(index, carry):
+        inner_blocks(index * blocks, blocks, x_ref, rate_ref, gain_ref, y_ref, mode_ref)
+        return carry
+
+    barrier = pltpu.get_barrier_semaphore()
+    for step in range(1, ctx_count):
+        pl.semaphore_signal(barrier, inc=1, device_id={"ctx": peer(step)}, device_id_type=MESH)
+    pl.semaphore_wait(barrier, ctx_count - 1)
+    first = []
+    for step in range(1, ctx_count):
+        first.append(
+            pltpu.make_async_remote_copy(
+                state_ref.at[peer(step)], near_ref.at[step], send_one.at[step], recv_one.at[step],
+                device_id={"ctx": peer(step)}, device_id_type=MESH,
+            )
+        )
+        first[-1].start()
+    near_ref[0] = state_ref[ctx]
+    lax.fori_loop(0, early, work, 0)
+    for copy in first:
+        copy.wait_recv()
+    scan_states(size, ctx, ctx_count, near_ref, own_ref, back_ref, extra_ref)
+    second = []
+    for step in range(1, ctx_count):
+        second.append(
+            pltpu.make_async_remote_copy(
+                back_ref.at[peer(step)], carry_ref.at[ctx], send_two.at[step], recv_two.at[step],
+                device_id={"ctx": peer(step)}, device_id_type=MESH,
+            )
+        )
+        second[-1].start()
+    carry_ref[ctx] = back_ref[ctx]
+    lax.fori_loop(early, rounds, work, 0)
+    for copy in second:
+        copy.wait_recv()
+    for copy in first + second:
+        copy.wait_send()
 
 
 def outer_kernel(
@@ -359,34 +463,30 @@
         name="states",
     )(proj, before, up, short_weight, rate_rows)
 
-    received = lax.all_to_all(
-        states.reshape(ctx_count, own_blocks, GROUP, 2 * LANES), "ctx", 0, 0, tiled=True
-    )
-
-    y, modes = pl.pallas_call(
-        functools.partial(inner_kernel, blocks),
-        grid=grid,
-        in_specs=[stacked(size, 2 * LANES), row_spec, row_spec],
-        out_specs=[stacked(size, 2 * LANES), stacked(8, LANES)],
-        out_shape=[array(block_count, size, 2 * LANES), array(block_count, 8, LANES)],
-        compiler_params=params,
-        cost_estimate=pl.CostEstimate(
-            flops=4 * block_count * 8 * size * size * LANES * 3,
-            bytes_accessed=block_count * size * 256 * 6,
-            transcendentals=block_count * size * LANES,
-        ),
-        name="inner",
-    )(x, rate_rows, gain_rows)
-
-    carry, extra = pl.pallas_call(
-        functools.partial(scan_kernel, size),
+    vmem = pl.BlockSpec(memory_space=pltpu.VMEM)
+    table = (ctx_count, own_blocks, GROUP, 2 * LANES)
+    y, modes, carry, extra = pl.pallas_call(
+        functools.partial(exchange_kernel, ctx_count, blocks, block_count // blocks // 2),
+        in_specs=[vmem] * 5,
+        out_specs=[vmem] * 4,
         out_shape=[
-            array(ctx_count, own_blocks, GROUP, 2 * LANES),
+            array(block_count, size, 2 * LANES),
+            array(block_count, 8, LANES),
+            array(*table),
             array(own_blocks, ROWS, LANES),
         ],
-        name="scan",
-    )(received, own_rates)
-    carry = lax.all_to_all(carry, "ctx", 0, 0, tiled=True).reshape(block_count, GROUP, 2 * LANES)
+        scratch_shapes=[
+            pltpu.VMEM(table, jnp.float32),
+            pltpu.VMEM(table, jnp.float32),
+            pltpu.SemaphoreType.DMA((ctx_count,)),
+            pltpu.SemaphoreType.DMA((ctx_count,)),
+            pltpu.SemaphoreType.DMA((ctx_count,)),
+            pltpu.SemaphoreType.DMA((ctx_count,)),
+        ],
+        compiler_params=pltpu.CompilerParams(collective_id=1, has_side_effects=True),
+        name="exchange",
+    )(states.reshape(table), x, rate_rows, gain_rows, own_rates)
+    carry = carry.reshape(block_count, GROUP, 2 * LANES)
 
     mixed, grad, first, last, part = pl.pallas_call(
         functools.partial(outer_kernel, blocks, norm),

time: 133 us -> 96.1 us (0.72)
  Pallas kernels: 91.1 us -> 75.4 us
  starting transfers between devices: 17.7 us -> 6.8 us
  waiting for transfers between devices: 9.11 us -> 1.5 us
  local copies, waits for them, and re-layouts: 12.1 us -> 9.19 us
    pallas_call x2 -> x1, Pallas kernels: 39.1 us -> 25.2 us  [local(): pl.pallas_call(functools.partial(exchange_kernel, ctx_count, blocks, bloc...]
    all_to_all x2 -> x0, starting transfers between devices: 10.9 us -> none  [the longest x1 6.23 us: local(): lax.all_to_all(states.reshape(ctx_count, own_blocks, GROUP, 2 * LANES), '...]
    all_to_all x2 -> x0, waiting for transfers between devices: 7.62 us -> none  [the longest x1 7.61 us: local(): lax.all_to_all(states.reshape(ctx_count, own_blocks, GROUP, 2 * LANES), '...]
    pallas_call x1, Pallas kernels: 25.1 us -> 23.2 us  [local(): pl.pallas_call(functools.partial(reduce_kernel, (dp_count, ctx_count, tp_...]
    unnamed x12 -> x10, local copies, waits for them, and re-layouts: 2.85 us -> 1.26 us
  transfers between devices with their start and end apart: 4 -> 2, of which waited for: 2 -> 1; matrix products, arithmetic and copies ran while one was open for 4% -> 5% of each run, Pallas kernels for 28% -> 0%
where the time goes in v2:
time: 96.1 us; the launch traced here: 95.2 us
  Pallas kernels  75.4 us (78%)
  local copies, waits for them, and re-layouts  9.19 us (10%)
  starting transfers between devices  6.8 us (7%)
  waiting for transfers between devices  1.5 us (2%)
  other arithmetic  1.46 us (2%)
    pallas_call x1, Pallas kernels, local(): pl.pallas_call(functools.partial(exchange_kernel, ctx_count, blocks, bloc...  25.2 us
    pallas_call x1, Pallas kernels, local(): pl.pallas_call(functools.partial(reduce_kernel, (dp_count, ctx_count, tp_...  23.2 us
    pallas_call x1, Pallas kernels, local(): pl.pallas_call(functools.partial(outer_kernel, blocks, norm), grid=grid,...  13.3 us
    pallas_call x1, Pallas kernels, local(): pl.pallas_call(functools.partial(gather_kernel, blocks), grid=grid, in_sp...  10.4 us
    ppermute x2, starting transfers between devices, shifted(): lax.ppermute(value, axis, [(source, source + steps) for source in range(l...  6.8 us
    pallas_call x1, Pallas kernels, local(): pl.pallas_call(mend_kernel, grid=(width // mend_width,), in_specs=[tail,...  3.29 us
    slice x1, local copies, waits for them, and re-layouts, both_halves(): mine = flat_sums[:, 10 + index].reshape(1, group_count, GROUP)  2.03 us
  transfers between devices with their start and end apart: 2, of which 1 were waited for; matrix products, arithmetic and copies ran while one was open for 5% of the time, Pallas kernels for 0%

profile of v2, /device:TPU:1, one launch (start us, length us, event | category | flops | bytes accessed | tf_op | source)
XLA Modules:
  0.0 95.2 jit_solution(17211610272765171224)
XLA Ops:
  0.6 1.0 %slice.32 = bf16[3,2,4096]{2,1,0:T(2,128)(2,1)S(1)} slice(bf16[3,128,4096]{2,1,0:T(8,128)(2,1)} %bitcast.32), slice={[0:3], [126:128], [0:4096]} | slice | bytes 98304 | tf_op jit(solution)/shard_map/slice | solution.py:424
  1.6 4.5 %collective-permute-start = (bf16[3,2,4096]{2,1,0:T(2,128)(2,1)S(1)}, bf16[3,2,4096]{2,1,0:T(2,128)(2,1)S(1)}, u32[]{:S(2)}, u32[]{:S(2)}) collective-permute-start(bf16[3,2,4096]{2,1,0:T(2,128)(2,1)S(1)} %slice.32), channel_id=1, source_target_pairs={{0,2},{2,4},{4,6},{6,8},{8,10},{10,12},{12,14},{14,16},{16,18},{18... | collective-permute-start | bytes 147464 | tf_op jit(solution)/shard_map/ppermute | solution.py:23
  6.1 0.7 sqrt_multiply_fusion.3
  6.9 0.1 copy.72
  7.0 0.1 reshape.131
  7.1 0.0 copy-start
  7.1 0.6 constant_dynamic-slice_fusion.own_ref
  7.7 0.1 copy.73
  7.8 0.7 reshape.132
  8.5 0.0 collective-permute-done.halo_ref
  8.5 0.0 copy-start.1
  8.5 0.0 copy-done
  8.5 0.6 copy-done.1
  9.1 10.4 %states.1 = (bf16[32,128,256]{2,1,0:T(8,128)(2,1)}, f32[32,16,256]{2,1,0:T(8,128)}, f32[32,16,256]{2,1,0:T(8,128)}) custom-call(bf16[3,128,4096]{2,1,0:T(8,128)(2,1)} %bitcast.33, bf16[3,2,4096]{2,1,0:T(2,128)(2,1)} %copy-done.1, bf16[128,4096]{1,0:T(8,128)(2,1)} %bitcast.35, f32[3,3,4096]{2,1,0:T(4,128)} %weight_ref.5, f32[32,1,128]{2,1,0:T(1,128)} %bitcast.45), custom_call_target="tpu_custom_call" | custom-call | tf_op jit(solution)/shard_map/states/pallas_call | solution.py:452
  19.5 25.2 %exchange.1 = (f32[32,128,256]{2,1,0:T(8,128)}, f32[32,8,128]{2,1,0:T(8,128)}, f32[16,2,16,256]{3,2,1,0:T(8,128)}, f32[2,16,128]{2,1,0:T(8,128)}) custom-call(f32[16,2,16,256]{3,2,1,0:T(8,128)} %bitcast.43, bf16[32,128,256]{2,1,0:T(8,128)(2,1)} %get-tuple-element.19.x_ref, f32[32,1,128]{2,1,0:T(1,128)} %bitcast.46, f32[32,1,128]{2,1,0:T(1,128)} %bitcast.49, ...), custom_call_target="tpu_custom_call" | custom-call | tf_op jit(solution)/shard_map/exchange/pallas_call | solution.py:468
  44.7 13.3 %outer.1 = (bf16[128,4096]{1,0:T(8,128)(2,1)}, bf16[3,128,4096]{2,1,0:T(8,128)(2,1)}, f32[3,8,4096]{2,1,0:T(8,128)}, f32[3,8,4096]{2,1,0:T(8,128)}, f32[32,16,128]{2,1,0:T(8,128)}) custom-call(bf16[3,128,4096]{2,1,0:T(8,128)(2,1)} %bitcast.34, bf16[3,2,4096]{2,1,0:T(2,128)(2,1)} %copy-done.1, bf16[128,4096]{1,0:T(8,128)(2,1)} %bitcast.36, ...), custom_call_target="tpu_custom_call" | custom-call | tf_op jit(solution)/shard_map/outer/pallas_call | solution.py:491
  58.0 0.0 copy-start.3
  58.0 0.0 copy-start.4
  58.1 23.2 %reduce.1 = f32[16,2,16,128]{3,2,1,0:T(8,128)} custom-call(f32[16,2,16,128]{3,2,1,0:T(8,128)} %bitcast.48, f32[2,16,128]{2,1,0:T(8,128)} %get-tuple-element.29.extra_ref), custom_call_target="tpu_custom_call" | custom-call | tf_op jit(solution)/shard_map/reduce/pallas_call | solution.py:513
  81.3 2.0 %fusion.6 = (f32[32,1,128]{2,1,0:T(1,128)S(1)}, f32[32,1,128]{2,1,0:T(1,128)S(1)}, f32[32,1,128]{2,1,0:T(1,128)S(1)}, f32[32,1,128]{2,1,0:T(1,128)S(1)}, f32[32,1,128]{2,1,0:T(1,128)}) fusion(f32[32,16,128]{2,1,0:T(8,128)} %bitcast.38), kind=kLoop, calls=%fused_computation.19 | loop fusion | bytes 163840 | tf_op jit(solution)/shard_map/slice | solution.py:557
  83.3 1.0 %slice_bitcast_fusion = f32[9,32,128]{2,0,1:T(8,128)S(1)} fusion(f32[32,16,128]{2,1,0:T(8,128)} %bitcast.39), kind=kLoop, calls=%fused_computation | loop fusion | bytes 294912 | tf_op jit(solution)/shard_map/transpose | solution.py:553
  84.3 1.0 %slice.25 = f32[3,2,4096]{2,1,0:T(2,128)S(1)} slice(f32[3,8,4096]{2,1,0:T(8,128)} %get-tuple-element.27), slice={[0:3], [0:2], [0:4096]} | slice | bytes 196608 | tf_op jit(solution)/shard_map/slice | solution.py:510
  85.3 2.3 %collective-permute-start.1 = (f32[3,2,4096]{2,1,0:T(2,128)S(1)}, f32[3,2,4096]{2,1,0:T(2,128)S(1)}, u32[]{:S(2)}, u32[]{:S(2)}) collective-permute-start(f32[3,2,4096]{2,1,0:T(2,128)S(1)} %slice.25), channel_id=1, source_target_pairs={{2,0},{4,2},{6,4},{8,6},{10,8},{12,10},{14,12},{16,14},{18,16},{20... | collective-permute-start | bytes 294920 | tf_op jit(solution)/shard_map/ppermute | solution.py:23
  87.6 0.1 select_n.79
  87.7 0.1 select_n.81
  87.9 0.1 copy.88
  88.0 0.1 select_n.77
  88.1 0.1 select_n.75
  88.2 0.1 copy.87
  88.3 0.0 copy-done.3
  88.3 0.0 copy-done.4
  88.3 0.7 fusion.4
  89.0 0.7 reshape.137
  89.8 1.5 %collective-permute-done.1.after_ref = f32[3,2,4096]{2,1,0:T(2,128)S(1)} collective-permute-done((f32[3,2,4096]{2,1,0:T(2,128)S(1)}, f32[3,2,4096]{2,1,0:T(2,128)S(1)}, u32[]{:S(2)}, u32[]{:S(2)}) %collective-permute-start.1) | collective-permute-done | bytes 98336 | tf_op jit(solution)/shard_map/ppermute | solution.py:23
  91.2 0.0 copy-start.2
  91.2 0.6 copy-done.2
  91.9 3.3 %mend.1 = bf16[3,128,4096]{2,1,0:T(8,128)(2,1)} custom-call(bf16[3,128,4096]{2,1,0:T(8,128)(2,1)} %get-tuple-element.25.grad_ref, f32[3,8,4096]{2,1,0:T(8,128)} %get-tuple-element.26.last_ref, f32[3,2,4096]{2,1,0:T(2,128)} %copy-done.2, f32[3,3,4096]{2,1,0:T(4,128)} %weight_ref.5), custom_call_target="tpu_custom_call", output_to_operand_aliasing={{}: (0, {})} | custom-call | tf_op jit(solution)/shard_map/mend/pallas_call | solution.py:536
  (4 shorter events, 0.1 us)
Async XLA Ops:
  1.6 6.9 %collective-permute-start = (bf16[3,2,4096]{2,1,0:T(2,128)(2,1)S(1)}, bf16[3,2,4096]{2,1,0:T(2,128)(2,1)S(1)}, u32[]{:S(2)}, u32[]{:S(2)}) collective-permute-start(bf16[3,2,4096]{2,1,0:T(2,128)(2,1)S(1)} %slice.32), channel_id=1, source_target_pairs={{0,2},{2,4},{4,6},{6,8},{8,10},{10,12},{12,14},{14,16},{16,18},{18... | collective-permute-start | bytes 147464 | tf_op jit(solution)/shard_map/ppermute | solution.py:23
  7.1 1.4 %copy-start = (f32[32,1,128]{2,0,1:T(8,128)}, f32[32,1,128]{2,0,1:T(8,128)S(1)}, u32[]{:S(2)}) copy-start(f32[32,1,128]{2,0,1:T(8,128)S(1)} %reshape.131) | copy-start | bytes 49156
  8.5 0.6 copy-start.1
  58.0 30.3 %copy-start.3 = (f32[512,16]{0,1:T(8,128)S(1)}, f32[512,16]{0,1:T(8,128)}, u32[]{:S(2)}) copy-start(f32[512,16]{0,1:T(8,128)} %param.10) | copy-start | bytes 98308
  58.0 30.3 %copy-start.4 = (f32[512,16]{0,1:T(8,128)S(1)}, f32[512,16]{0,1:T(8,128)}, u32[]{:S(2)}) copy-start(f32[512,16]{0,1:T(8,128)} %param.11) | copy-start | bytes 98308
  85.3 5.9 %collective-permute-start.1 = (f32[3,2,4096]{2,1,0:T(2,128)S(1)}, f32[3,2,4096]{2,1,0:T(2,128)S(1)}, u32[]{:S(2)}, u32[]{:S(2)}) collective-permute-start(f32[3,2,4096]{2,1,0:T(2,128)S(1)} %slice.25), channel_id=1, source_target_pairs={{2,0},{4,2},{6,4},{8,6},{10,8},{12,10},{14,12},{16,14},{18,16},{20... | collective-permute-start | bytes 294920 | tf_op jit(solution)/shard_map/ppermute | solution.py:23
  91.2 0.6 copy-start.2

commit v3 on v2

--- a/solution.py
+++ b/solution.py
@@ -275,10 +275,36 @@
 
 
 def outer_kernel(
-    blocks, norm, proj_ref, halo_ref, up_ref, weight_ref, skip_ref, rate_ref, gain_ref, y_ref,
-    carry_ref, slope_ref, mode_ref, mixed_ref, grad_ref, first_ref, last_ref, part_ref,
+    counts, blocks, norm, proj_ref, halo_ref, up_ref, weight_ref, skip_ref, rate_ref, gain_ref, y_ref,
+    carry_ref, slope_ref, mode_ref, extra_ref, mixed_ref, grad_ref, after_ref, last_ref, out_ref,
+    part_ref, head_ref, next_ref, near_ref, sum_ref, far_ref, done_ref, all_ref,
+    send_one, recv_one, send_two, recv_two, send_three, recv_three, send_head, recv_head,
 ):
+    dp_count, ctx_count, tp_count = counts
+    dp, ctx, tp = lax.axis_index("dp"), lax.axis_index("ctx"), lax.axis_index("tp")
+    others = [(a, b) for b in range(tp_count) for a in range(dp_count) if (a, b) != (0, 0)]
+    own_blocks = part_ref.shape[1]
+    owners = blocks // own_blocks
+    index = pl.program_id(0)
+    rounds = pl.num_programs(0)
+    place = lax.rem(index + ctx // owners, rounds)
     size = proj_ref.shape[1]
+
+    def peer(step):
+        return lax.rem(ctx + step, ctx_count)
+
+    def cross(pair):
+        return {"dp": lax.rem(dp + pair[0], dp_count), "tp": lax.rem(tp + pair[1], tp_count)}
+
+    barrier = pltpu.get_barrier_semaphore()
+
+    @pl.when(index == 0)
+    def _():
+        for step in range(1, ctx_count):
+            pl.semaphore_signal(barrier, inc=1, device_id={"ctx": peer(step)}, device_id_type=MESH)
+        for pair in others:
+            pl.semaphore_signal(barrier, inc=1, device_id=cross(pair), device_id_type=MESH)
+
     row = iota((size, LANES), 0)
     keep = iota((LANES, 2 * LANES), 0) // GROUP == iota((LANES, 2 * LANES), 1) % LANES // GROUP
     ages = (iota((size, LANES), 0) + 1).astype(jnp.float32)
@@ -303,16 +329,21 @@
         mixed_ref[:, lanes] = (query * mixture).astype(jnp.bfloat16)
         grad_gate = correlated + skip * grad_sum
         lines = []
+        heads = []
+        lasts = []
         for part, grads in enumerate((upstream * mixture, grad_gate * value, grad_gate * key)):
             weight = weight_ref[part, :, lanes]
             ahead = jnp.where(row < size - 1, pltpu.roll(grads, size - 1, 0), 0.0)
             further = jnp.where(row < size - 2, pltpu.roll(grads, size - 2, 0), 0.0)
             result = grads * weight[0:1] + ahead * weight[1:2] + further * weight[2:3]
             grad_ref[part, :, lanes] = result.astype(jnp.bfloat16)
-            first_ref[part, :, lanes] = grads[:8]
-            last_ref[part, :, lanes] = result[size - 8 :]
+            heads.append(grads[:2])
+            lasts.append(result[size - 2 :])
             for tap in taps[part]:
                 lines.append(jnp.sum(grads * tap, axis=0, keepdims=True) * norm)
+        blank = jnp.zeros((2, LANES), jnp.float32)
+        head_ref[index, :, lanes] = jnp.concatenate(heads + [blank], axis=0)
+        last_ref[:, lanes] = jnp.concatenate(lasts + [blank], axis=0)
         lines.append(jnp.sum(grad_sum * gated, axis=0, keepdims=True) * norm)
         slopes = slope_ref[block]
         between = slopes[:, LANES:] * carry[:, :LANES] + slopes[:, :LANES] * carry[:, LANES:]
@@ -320,93 +351,111 @@
         lines.append(modes[0:1])
         lines.append(modes[1:2] + jnp.exp(-rate_row) * to_row(between))
         lines.append(jnp.zeros((4, LANES), jnp.float32))
-        part_ref[block] = jnp.concatenate(lines, axis=0)
-
-
-def mend_kernel(grad_ref, last_ref, after_ref, weight_ref, out_ref):
+        part_ref[place * owners + block // own_blocks, block % own_blocks] = jnp.concatenate(lines, axis=0)
+
+    @pl.when(index == 0)
+    def _():
+        pl.semaphore_wait(barrier, ctx_count - 1 + len(others))
+
+    def first_copy(owner, source):
+        return pltpu.make_async_remote_copy(
+            part_ref.at[owner], near_ref.at[source], send_one.at[owner], recv_one.at[source],
+            device_id={"ctx": owner}, device_id_type=MESH,
+        )
+
+    def head_copy(at):
+        return pltpu.make_async_remote_copy(
+            head_ref.at[at], next_ref.at[at], send_head.at[at], recv_head.at[at],
+            device_id={"ctx": lax.rem(ctx + ctx_count - 1, ctx_count)}, device_id_type=MESH,
+        )
+
+    for item in range(owners):
+        owner = place * owners + item
+
+        @pl.when(owner != ctx)
+        def _():
+            first_copy(owner, ctx).start()
+
+    head_copy(index).start()
+
+    @pl.when(index == rounds - 1)
+    def _():
+        total = part_ref[ctx] + extra_ref[...]
+        for step in range(1, ctx_count):
+            first_copy(ctx, peer(step)).wait_recv()
+            total = total + near_ref[peer(step)]
+        sum_ref[...] = total
+        second = []
+        for number, pair in enumerate(others):
+            second.append(
+                pltpu.make_async_remote_copy(
+                    sum_ref, far_ref.at[number], send_two.at[number], recv_two.at[number],
+                    device_id=cross(pair), device_id_type=MESH,
+                )
+            )
+            second[-1].start()
+        foreign = jnp.zeros_like(total)
+        for number, pair in enumerate(others):
+            second[number].wait_recv()
+            if pair[1] == 0:
+                total = total + far_ref[number]
+            else:
+                foreign = foreign + far_ref[number]
+        line = iota(total.shape, 1)
+        low = jnp.where(tp == 0, total, foreign)
+        high = pltpu.roll(jnp.where(tp == 0, foreign, total), 2, 1)
+        total = jnp.where(line < 10, total, jnp.where(line < 12, low, high))
+        done_ref[...] = total
+        third = []
+        for step in range(1, ctx_count):
+            third.append(
+                pltpu.make_async_remote_copy(
+                    done_ref, all_ref.at[ctx], send_three.at[step], recv_three.at[step],
+                    device_id={"ctx": peer(step)}, device_id_type=MESH,
+                )
+            )
+            third[-1].start()
+        all_ref[ctx] = total
+        width = blocks * LANES
+        for at in range(part_ref.shape[0] // owners):
+            head_copy(at).wait_recv()
+            spot = lax.rem(at + lax.rem(ctx + 1, ctx_count) // owners, part_ref.shape[0] // owners)
+            rows = next_ref[at]
+            after_ref[:, pl.ds(pl.multiple_of(spot * width, LANES), width)] = jnp.where(
+                ctx < ctx_count - 1, rows, jnp.zeros_like(rows)
+            )
+        for copy in third:
+            copy.wait_recv()
+        out_ref[...] = all_ref[...]
+        for step in range(1, ctx_count):
+            first_copy(peer(step), ctx).wait_send()
+        for at in range(part_ref.shape[0] // owners):
+            head_copy(at).wait_send()
+        for copy in second + third:
+            copy.wait_send()
+
+
+def finish_kernel(
+    blocks, grad_ref, mixed_ref, after_ref, last_ref, weight_ref, sum_ref, grad_out, mixed_out, short_out,
+    skip_out,
+):
+    mixed_out[...] = mixed_ref[...]
+    size = grad_ref.shape[1]
     for part in range(3):
-        tile = grad_ref[part]
-        last = last_ref[part]
-        after = after_ref[part]
         weight = weight_ref[part]
-        late = last[6:7] + after[0:1] * weight[2:3]
-        final = last[7:8] + after[0:1] * weight[1:2] + after[1:2] * weight[2:3]
+        after = after_ref[2 * part : 2 * part + 2]
+        late = last_ref[2 * part : 2 * part + 1] + after[0:1] * weight[2:3]
+        final = last_ref[2 * part + 1 : 2 * part + 2] + after[0:1] * weight[1:2] + after[1:2] * weight[2:3]
+        grad_out[part, : size - 16] = grad_ref[part, : size - 16]
+        tile = grad_ref[part, size - 16 :].astype(jnp.float32)
         row = iota(tile.shape, 0)
-        wide = jnp.where(row == 14, late, jnp.where(row == 15, final, tile.astype(jnp.float32)))
-        out_ref[part] = wide.astype(jnp.bfloat16)
-
-
-def reduce_kernel(
-    counts, part_ref, extra_ref, out_ref, near_ref, sum_ref, far_ref, done_ref,
-    send_one, recv_one, send_two, recv_two, send_three, recv_three,
-):
-    dp_count, ctx_count, tp_count = counts
-    dp, ctx, tp = lax.axis_index("dp"), lax.axis_index("ctx"), lax.axis_index("tp")
-    others = [(a, b) for b in range(tp_count) for a in range(dp_count) if (a, b) != (0, 0)]
-
-    def ring(step):
-        return {"ctx": lax.rem(ctx + step, ctx_count)}
-
-    def cross(pair):
-        return {"dp": lax.rem(dp + pair[0], dp_count), "tp": lax.rem(tp + pair[1], tp_count)}
-
-    barrier = pltpu.get_barrier_semaphore()
-    for step in range(1, ctx_count):
-        pl.semaphore_signal(barrier, inc=1, device_id=ring(step), device_id_type=MESH)
-    for pair in others:
-        pl.semaphore_signal(barrier, inc=1, device_id=cross(pair), device_id_type=MESH)
-    pl.semaphore_wait(barrier, ctx_count - 1 + len(others))
-
-    first = []
-    for step in range(1, ctx_count):
-        first.append(
-            pltpu.make_async_remote_copy(
-                part_ref.at[lax.rem(ctx + step, ctx_count)], near_ref.at[step],
-                send_one.at[step], recv_one.at[step], device_id=ring(step), device_id_type=MESH,
-            )
-        )
-        first[-1].start()
-    total = part_ref[ctx] + extra_ref[...]
-    for step in range(1, ctx_count):
-        first[step - 1].wait_recv()
-        total = total + near_ref[step]
-    sum_ref[...] = total
-
-    second = []
-    for index, pair in enumerate(others):
-        second.append(
-            pltpu.make_async_remote_copy(
-                sum_ref, far_ref.at[index], send_two.at[index], recv_two.at[index],
-                device_id=cross(pair), device_id_type=MESH,
-            )
-        )
-        second[-1].start()
-    foreign = jnp.zeros_like(total)
-    for index, pair in enumerate(others):
-        second[index].wait_recv()
-        if pair[1] == 0:
-            total = total + far_ref[index]
-        else:
-            foreign = foreign + far_ref[index]
-    moved = pltpu.roll(foreign, 2, 1)
-    row = iota(total.shape, 1)
-    total = jnp.where((row == 12) | (row == 13), moved, total)
-    done_ref[...] = total
-
-    third = []
-    for step in range(1, ctx_count):
-        third.append(
-            pltpu.make_async_remote_copy(
-                done_ref, out_ref.at[ctx], send_three.at[step], recv_three.at[step],
-                device_id=ring(step), device_id_type=MESH,
-            )
-        )
-        third[-1].start()
-    out_ref[ctx] = total
-    for copy in third:
-        copy.wait_recv()
-    for copy in first + second + third:
-        copy.wait_send()
+        tile = jnp.where(row == 14, late, jnp.where(row == 15, final, tile))
+        grad_out[part, size - 16 :] = tile.astype(jnp.bfloat16)
+    for block in range(blocks):
+        lanes = pl.ds(block * LANES, LANES)
+        for part in range(3):
+            short_out[part, :, lanes] = sum_ref[block, 3 * part : 3 * part + 3]
+        skip_out[:, lanes] = sum_ref[block, 9:10]
 
 
 def local(projected, upstream, short_weight, skip_gain, residues, rates):
@@ -435,7 +484,6 @@
     step_width = blocks * LANES
     wide3 = pl.BlockSpec((3, size, step_width), lambda i: (0, 0, i))
     halo3 = pl.BlockSpec((3, 2, step_width), lambda i: (0, 0, i))
-    tile3 = pl.BlockSpec((3, 8, step_width), lambda i: (0, 0, i))
     taps3 = pl.BlockSpec((3, 3, step_width), lambda i: (0, 0, i))
     flat = pl.BlockSpec((size, step_width), lambda i: (0, i))
     line = pl.BlockSpec((1, step_width), lambda i: (0, i))
@@ -488,82 +536,91 @@
     )(states.reshape(table), x, rate_rows, gain_rows, own_rates)
     carry = carry.reshape(block_count, GROUP, 2 * LANES)
 
-    mixed, grad, first, last, part = pl.pallas_call(
-        functools.partial(outer_kernel, blocks, norm),
+    owners = blocks // own_blocks
+    rounds = block_count // blocks
+    others = max(dp_count * tp_count - 1, 1)
+    own = (own_blocks, ROWS, LANES)
+
+    def turned(rank, at):
+        def index_map(i):
+            spot = lax.rem(i + lax.axis_index("ctx") // owners, rounds)
+            return tuple(spot if d == at else 0 for d in range(rank))
+
+        return index_map
+
+    def lane_spec(*shape):
+        return pl.BlockSpec(shape + (step_width,), turned(len(shape) + 1, len(shape)))
+
+    def block_spec(rows, cols):
+        return pl.BlockSpec((blocks, rows, cols), turned(3, 0))
+
+    def whole(*shape):
+        return pl.BlockSpec(shape, lambda i: (0,) * len(shape))
+
+    mixed, grad, after, last, summed = pl.pallas_call(
+        functools.partial(outer_kernel, (dp_count, ctx_count, tp_count), blocks, norm),
         grid=grid,
         in_specs=[
-            wide3, halo3, flat, taps3, line, row_spec, row_spec, stacked(size, 2 * LANES),
-            stacked(GROUP, 2 * LANES), stacked(GROUP, 2 * LANES), stacked(8, LANES),
-        ],
-        out_specs=[flat, wide3, tile3, tile3, stacked(ROWS, LANES)],
+            lane_spec(3, size), lane_spec(3, 2), lane_spec(size), lane_spec(3, 3), lane_spec(1),
+            block_spec(1, LANES), block_spec(1, LANES), block_spec(size, 2 * LANES),
+            block_spec(GROUP, 2 * LANES), block_spec(GROUP, 2 * LANES), block_spec(8, LANES),
+            whole(*own),
+        ],
+        out_specs=[
+            lane_spec(size), lane_spec(3, size), whole(8, width), lane_spec(8), whole(ctx_count, *own)
+        ],
         out_shape=[
             array(size, width, kind=jnp.bfloat16),
             array(3, size, width, kind=jnp.bfloat16),
-            array(3, 8, width),
-            array(3, 8, width),
-            array(block_count, ROWS, LANES),
+            array(8, width),
+            array(8, width),
+            array(ctx_count, *own),
+        ],
+        scratch_shapes=[
+            pltpu.VMEM((ctx_count,) + own, jnp.float32),
+            pltpu.VMEM((rounds, 8, step_width), jnp.float32),
+            pltpu.VMEM((rounds, 8, step_width), jnp.float32),
+            pltpu.VMEM((ctx_count,) + own, jnp.float32),
+            pltpu.VMEM(own, jnp.float32),
+            pltpu.VMEM((others,) + own, jnp.float32),
+            pltpu.VMEM(own, jnp.float32),
+            pltpu.VMEM((ctx_count,) + own, jnp.float32),
+            pltpu.SemaphoreType.DMA((ctx_count,)),
+            pltpu.SemaphoreType.DMA((ctx_count,)),
+            pltpu.SemaphoreType.DMA((others,)),
+            pltpu.SemaphoreType.DMA((others,)),
+            pltpu.SemaphoreType.DMA((ctx_count,)),
+            pltpu.SemaphoreType.DMA((ctx_count,)),
+            pltpu.SemaphoreType.DMA((rounds,)),
+            pltpu.SemaphoreType.DMA((rounds,)),
+        ],
+        compiler_params=pltpu.CompilerParams(
+            dimension_semantics=("arbitrary",), collective_id=0, has_side_effects=True
+        ),
+        name="outer",
+    )(proj, before, up, short_weight, skip_row, rate_rows, gain_rows, y, carry, slopes, modes, extra)
+    summed = summed.reshape(block_count, ROWS, LANES)
+
+    eight = pl.BlockSpec((8, step_width), lambda i: (0, i))
+    grad, mixed, grad_short, grad_skip = pl.pallas_call(
+        functools.partial(finish_kernel, blocks),
+        grid=grid,
+        in_specs=[wide3, flat, eight, eight, taps3, stacked(ROWS, LANES)],
+        out_specs=[wide3, flat, taps3, line],
+        out_shape=[
+            array(3, size, width, kind=jnp.bfloat16),
+            array(size, width, kind=jnp.bfloat16),
+            array(3, 3, width),
+            array(1, width),
         ],
         compiler_params=params,
-        name="outer",
-    )(proj, before, up, short_weight, skip_row, rate_rows, gain_rows, y, carry, slopes, modes)
-
-    after = shifted(first[:, :2], "ctx", -1)
-
-    others = dp_count * tp_count - 1
-    summed = pl.pallas_call(
-        functools.partial(reduce_kernel, (dp_count, ctx_count, tp_count)),
-        in_specs=[pl.BlockSpec(memory_space=pltpu.VMEM)] * 2,
-        out_specs=pl.BlockSpec(memory_space=pltpu.VMEM),
-        out_shape=array(ctx_count, own_blocks, ROWS, LANES),
-        scratch_shapes=[
-            pltpu.VMEM((ctx_count, own_blocks, ROWS, LANES), jnp.float32),
-            pltpu.VMEM((own_blocks, ROWS, LANES), jnp.float32),
-            pltpu.VMEM((max(others, 1), own_blocks, ROWS, LANES), jnp.float32),
-            pltpu.VMEM((own_blocks, ROWS, LANES), jnp.float32),
-            pltpu.SemaphoreType.DMA((ctx_count,)),
-            pltpu.SemaphoreType.DMA((ctx_count,)),
-            pltpu.SemaphoreType.DMA((max(others, 1),)),
-            pltpu.SemaphoreType.DMA((max(others, 1),)),
-            pltpu.SemaphoreType.DMA((ctx_count,)),
-            pltpu.SemaphoreType.DMA((ctx_count,)),
-        ],
-        compiler_params=pltpu.CompilerParams(collective_id=0, has_side_effects=True),
-        name="reduce",
-    )(part.reshape(ctx_count, own_blocks, ROWS, LANES), extra)
-
-    mend_width = math.gcd(width, 1024)
-    tail = pl.BlockSpec((3, 16, mend_width), lambda i: (0, size // 16 - 1, i))
-    grad = pl.pallas_call(
-        mend_kernel,
-        grid=(width // mend_width,),
-        in_specs=[
-            tail,
-            pl.BlockSpec((3, 8, mend_width), lambda i: (0, 0, i)),
-            pl.BlockSpec((3, 2, mend_width), lambda i: (0, 0, i)),
-            pl.BlockSpec((3, 3, mend_width), lambda i: (0, 0, i)),
-        ],
-        out_specs=tail,
-        out_shape=array(3, size, width, kind=jnp.bfloat16),
-        input_output_aliases={0: 0},
-        compiler_params=params,
-        name="mend",
-    )(grad, last, after, short_weight)
-
-    flat_sums = summed.reshape(block_count, ROWS, LANES)
-    grad_short = flat_sums[:, :9].transpose(1, 0, 2).reshape(3, 3, width)
-    grad_skip = flat_sums[:, 9].reshape(width)
-
-    def both_halves(index):
-        mine = flat_sums[:, 10 + index].reshape(1, group_count, GROUP)
-        if tp_count == 1:
-            return mine.reshape(group_count, GROUP)
-        other = flat_sums[:, 12 + index].reshape(1, group_count, GROUP)
-        low = jnp.where(tp == 0, mine, other)
-        high = jnp.where(tp == 0, other, mine)
-        return jnp.concatenate([low, high], axis=0).reshape(2 * group_count, GROUP)
-
-    sum_plain = both_halves(0)
-    sum_weighted = both_halves(1)
+        name="finish",
+    )(grad, mixed, after, last, short_weight, summed)
+
+    modes = summed[:, 10 : 10 + 2 * tp_count].reshape(block_count, tp_count, 2, PER_BLOCK, GROUP)
+    sum_plain, sum_weighted = (
+        modes[:, :, index].transpose(1, 0, 2, 3).reshape(tp_count * group_count, GROUP) for index in range(2)
+    )
     root = jnp.sqrt(rates)
     grad_residues = root * sum_plain * norm
     grad_log_rates = residues * (0.5 * root * sum_plain - rates * root * sum_weighted) * norm
@@ -571,7 +628,7 @@
         mixed[None],
         grad.transpose(1, 0, 2)[None],
         grad_short,
-        grad_skip,
+        grad_skip.reshape(width),
         grad_residues,
         grad_log_rates,
     )

time: 96.1 us -> 89.3 us (0.929)
  local copies, waits for them, and re-layouts: 9.19 us -> 4.76 us
  starting transfers between devices: 6.8 us -> 4.5 us
  Pallas kernels: 75.4 us -> 77.3 us
  waiting for transfers between devices: 1.5 us -> 0.01 us
    ppermute x2 -> x1, starting transfers between devices: 6.8 us -> 4.5 us  [shifted(): lax.ppermute(value, axis, [(source, source + steps) for source in range(l...]
    slice x2, local copies, waits for them, and re-layouts: 3.05 us -> 1.05 us  [local(): summed[:, 10:10 + 2 * tp_count]]
    pallas_call x3 -> x2, Pallas kernels: 39.9 us -> 41.6 us  [the longest x1 34.7 us: local(): pl.pallas_call(functools.partial(outer_kernel, (dp_count, ctx_count, tp_c...]
    ppermute x2 -> x1, waiting for transfers between devices: 1.5 us -> 0.01 us  [shifted(): lax.ppermute(value, axis, [(source, source + steps) for source in range(l...]
  transfers between devices with their start and end apart: 2 -> 1, of which waited for: 1 -> 0; matrix products, arithmetic and copies ran while one was open for 5% -> 3% of each run, Pallas kernels for 0% -> 0%
where the time goes in v3:
time: 89.3 us; the launch traced here: 88.7 us
  Pallas kernels  77.3 us (87%)
  local copies, waits for them, and re-layouts  4.76 us (5%)
  starting transfers between devices  4.5 us (5%)
  other arithmetic  1.41 us (2%)
    pallas_call x1, Pallas kernels, local(): pl.pallas_call(functools.partial(outer_kernel, (dp_count, ctx_count, tp_c...  34.7 us
    pallas_call x1, Pallas kernels, local(): pl.pallas_call(functools.partial(exchange_kernel, ctx_count, blocks, bloc...  25.3 us
    pallas_call x1, Pallas kernels, local(): pl.pallas_call(functools.partial(gather_kernel, blocks), grid=grid, in_sp...  10.4 us
    pallas_call x1, Pallas kernels, local(): pl.pallas_call(functools.partial(finish_kernel, blocks), grid=grid, in_sp...  6.89 us
    ppermute x1, starting transfers between devices, shifted(): lax.ppermute(value, axis, [(source, source + steps) for source in range(l...  4.5 us
  transfers between devices with their start and end apart: 1, of which 0 were waited for; matrix products, arithmetic and copies ran while one was open for 3% of the time, Pallas kernels for 0%

profile of v3, /device:TPU:1, one launch (start us, length us, event | category | flops | bytes accessed | tf_op | source)
XLA Modules:
  0.0 88.7 jit_solution(81977960089938997)
XLA Ops:
  0.6 1.0 %slice.16 = bf16[3,2,4096]{2,1,0:T(2,128)(2,1)S(1)} slice(bf16[3,128,4096]{2,1,0:T(8,128)(2,1)} %bitcast.26), slice={[0:3], [126:128], [0:4096]} | slice | bytes 98304 | tf_op jit(solution)/shard_map/slice | solution.py:473
  1.6 4.5 %collective-permute-start = (bf16[3,2,4096]{2,1,0:T(2,128)(2,1)S(1)}, bf16[3,2,4096]{2,1,0:T(2,128)(2,1)S(1)}, u32[]{:S(2)}, u32[]{:S(2)}) collective-permute-start(bf16[3,2,4096]{2,1,0:T(2,128)(2,1)S(1)} %slice.16), channel_id=1, source_target_pairs={{0,2},{2,4},{4,6},{6,8},{8,10},{10,12},{12,14},{14,16},{16,18},{18... | collective-permute-start | bytes 147464 | tf_op jit(solution)/shard_map/ppermute | solution.py:23
  6.1 0.7 sqrt_multiply_fusion.3
  6.9 0.1 copy.32
  7.0 0.1 reshape.43
  7.1 0.0 copy-start
  7.1 0.6 constant_dynamic-slice_fusion.own_ref
  7.7 0.1 copy.33
  7.8 0.7 reshape.44
  8.5 0.0 collective-permute-done.halo_ref
  8.5 0.0 copy-start.1
  8.5 0.0 copy-done
  8.5 0.6 copy-done.1
  9.1 10.4 %states.1 = (bf16[32,128,256]{2,1,0:T(8,128)(2,1)}, f32[32,16,256]{2,1,0:T(8,128)}, f32[32,16,256]{2,1,0:T(8,128)}) custom-call(bf16[3,128,4096]{2,1,0:T(8,128)(2,1)} %bitcast.27, bf16[3,2,4096]{2,1,0:T(2,128)(2,1)} %copy-done.1, bf16[128,4096]{1,0:T(8,128)(2,1)} %bitcast.29, f32[3,3,4096]{2,1,0:T(4,128)} %weight_ref.5, f32[32,1,128]{2,1,0:T(1,128)} %bitcast.39), custom_call_target="tpu_custom_call" | custom-call | tf_op jit(solution)/shard_map/states/pallas_call | solution.py:500
  19.5 25.3 %exchange.1 = (f32[32,128,256]{2,1,0:T(8,128)}, f32[32,8,128]{2,1,0:T(8,128)}, f32[16,2,16,256]{3,2,1,0:T(8,128)}, f32[2,16,128]{2,1,0:T(8,128)}) custom-call(f32[16,2,16,256]{3,2,1,0:T(8,128)} %bitcast.35, bf16[32,128,256]{2,1,0:T(8,128)(2,1)} %get-tuple-element.23.x_ref, f32[32,1,128]{2,1,0:T(1,128)} %bitcast.40, f32[32,1,128]{2,1,0:T(1,128)} %bitcast.42, ...), custom_call_target="tpu_custom_call" | custom-call | tf_op jit(solution)/shard_map/exchange/pallas_call | solution.py:516
  44.8 0.0 copy-start.2
  44.8 0.0 copy-start.3
  44.8 34.7 %outer.1 = (bf16[128,4096]{1,0:T(8,128)(2,1)}, bf16[3,128,4096]{2,1,0:T(8,128)(2,1)}, f32[8,4096]{1,0:T(8,128)}, f32[8,4096]{1,0:T(8,128)}, f32[16,2,16,128]{3,2,1,0:T(8,128)}) custom-call(bf16[3,128,4096]{2,1,0:T(8,128)(2,1)} %bitcast.28, bf16[3,2,4096]{2,1,0:T(2,128)(2,1)} %copy-done.1, bf16[128,4096]{1,0:T(8,128)(2,1)} %bitcast.30, ...), custom_call_target="tpu_custom_call" | custom-call | tf_op jit(solution)/shard_map/outer/pallas_call | solution.py:560
  79.5 0.9 %slice.17 = f32[32,4,128]{2,1,0:T(4,128)S(1)} slice(f32[32,16,128]{2,1,0:T(8,128)} %bitcast.36), slice={[0:32], [10:14], [0:128]} | slice | bytes 131072 | tf_op jit(solution)/shard_map/slice | solution.py:620
  80.4 0.1 copy.40
  80.6 0.1 copy.44
  80.8 0.1 copy.45
  80.9 0.2 copy.41
  81.0 0.1 copy.42
  81.1 0.0 copy-done.2
  81.1 0.0 copy-done.3
  81.1 0.7 fusion.4
  81.8 6.9 %finish.1 = (bf16[3,128,4096]{2,1,0:T(8,128)(2,1)}, bf16[128,4096]{1,0:T(8,128)(2,1)}, f32[3,3,4096]{2,1,0:T(4,128)}, f32[1,4096]{1,0:T(1,128)}) custom-call(bf16[3,128,4096]{2,1,0:T(8,128)(2,1)} %get-tuple-element.29.grad_ref, bf16[128,4096]{1,0:T(8,128)(2,1)} %get-tuple-element.30.mixed_ref, f32[8,4096]{1,0:T(8,128)} %get-tuple-element.31.after_ref, ...), custom_call_target="tpu_custom_call" | custom-call | tf_op jit(solution)/shard_map/finish/pallas_call | solution.py:605
  (1 shorter events, 0.0 us)
Async XLA Ops:
  1.6 6.9 %collective-permute-start = (bf16[3,2,4096]{2,1,0:T(2,128)(2,1)S(1)}, bf16[3,2,4096]{2,1,0:T(2,128)(2,1)S(1)}, u32[]{:S(2)}, u32[]{:S(2)}) collective-permute-start(bf16[3,2,4096]{2,1,0:T(2,128)(2,1)S(1)} %slice.16), channel_id=1, source_target_pairs={{0,2},{2,4},{4,6},{6,8},{8,10},{10,12},{12,14},{14,16},{16,18},{18... | collective-permute-start | bytes 147464 | tf_op jit(solution)/shard_map/ppermute | solution.py:23
  7.1 1.4 %copy-start = (f32[32,1,128]{2,0,1:T(8,128)}, f32[32,1,128]{2,0,1:T(8,128)S(1)}, u32[]{:S(2)}) copy-start(f32[32,1,128]{2,0,1:T(8,128)S(1)} %reshape.43) | copy-start | bytes 49156
  8.5 0.6 copy-start.1
  44.8 36.4 %copy-start.2 = (f32[512,16]{0,1:T(8,128)S(1)}, f32[512,16]{0,1:T(8,128)}, u32[]{:S(2)}) copy-start(f32[512,16]{0,1:T(8,128)} %param.10) | copy-start | bytes 98308
  44.8 36.4 %copy-start.3 = (f32[512,16]{0,1:T(8,128)S(1)}, f32[512,16]{0,1:T(8,128)}, u32[]{:S(2)}) copy-start(f32[512,16]{0,1:T(8,128)} %param.11) | copy-start | bytes 98308

commit v4 on v3

--- a/solution.py
+++ b/solution.py
@@ -11,7 +11,6 @@
 GROUP = 16
 LANES = 128
 PER_BLOCK = LANES // GROUP
-PRECISE = lax.Precision.HIGHEST
 MESH = pl.DeviceIdType.MESH
 ROWS = 16
 SUB = 32
@@ -32,6 +31,13 @@
     return high, (value - high.astype(jnp.float32)).astype(jnp.bfloat16)
 
 
+def thirds(value):
+    high = value.astype(jnp.bfloat16)
+    rest = value - high.astype(jnp.float32)
+    middle = rest.astype(jnp.bfloat16)
+    return high, middle, (rest - middle.astype(jnp.float32)).astype(jnp.bfloat16)
+
+
 def dot(left, right, dims=((1,), (0,)), precision=None):
     return lax.dot_general(
         left, right, (dims, ((), ())), precision=precision, preferred_element_type=jnp.float32
@@ -48,58 +54,66 @@
     return table, ages * table
 
 
+def group_dot(value):
+    rows = iota((3 * LANES, LANES), 0)
+    cols = iota((3 * LANES, LANES), 1)
+    same = (rows % LANES // GROUP == cols // GROUP).astype(jnp.bfloat16)
+    return dot(jnp.concatenate(thirds(value), axis=1), same)
+
+
 def to_row(value):
-    rows = iota((LANES, LANES), 0)
-    cols = iota((LANES, LANES), 1)
-    same = (rows // GROUP == cols // GROUP).astype(jnp.float32)
-    summed = dot(value, same, precision=PRECISE)
     pick = iota(value.shape, 0) == iota(value.shape, 1) % GROUP
-    return jnp.sum(jnp.where(pick, summed, 0.0), axis=0, keepdims=True)
+    return jnp.sum(jnp.where(pick, group_dot(value), 0.0), axis=0, keepdims=True)
 
 
 def to_wide(rate_row):
-    rows = iota((LANES, LANES), 0)
-    cols = iota((LANES, LANES), 1)
-    same = (rows // GROUP == cols // GROUP).astype(jnp.float32)
     pick = iota((GROUP, LANES), 0) == iota((GROUP, LANES), 1) % GROUP
-    return dot(jnp.where(pick, jnp.broadcast_to(rate_row, (GROUP, LANES)), 0.0), same, precision=PRECISE)
-
-
-def delayed(value, halo):
-    row = iota(value.shape, 0)
-    one = jnp.where(row == 0, halo[1:2], pltpu.roll(value, 1, 0))
-    two = jnp.where(row == 0, halo[0:1], jnp.where(row == 1, halo[1:2], pltpu.roll(value, 2, 0)))
-    return one, two
-
-
-def features_of(proj_ref, halo_ref, weight_ref, lanes):
+    return group_dot(jnp.where(pick, jnp.broadcast_to(rate_row, (GROUP, LANES)), 0.0))
+
+
+def features_of(proj_ref, halo_ref, weight_ref, pad_ref, lanes, zero):
     outs = []
     taps = []
+    size = proj_ref.shape[1]
     for part in range(3):
         now = proj_ref[part, :, lanes].astype(jnp.float32)
         halo = halo_ref[part, :, lanes].astype(jnp.float32)
-        one, two = delayed(now, halo)
+        pad_ref[part, 0:8] = jnp.concatenate([jnp.zeros((6, LANES), jnp.float32), halo], axis=0)
+        pad_ref[part, 8:] = now
+        one = pad_ref[part, pl.ds(zero + 7, size)]
+        two = pad_ref[part, pl.ds(zero + 6, size)]
         weight = weight_ref[part, :, lanes]
         outs.append(now * weight[0:1] + one * weight[1:2] + two * weight[2:3])
         taps.append((now, one, two))
     return outs, taps
 
 
-def gather_kernel(blocks, proj_ref, halo_ref, up_ref, weight_ref, rate_ref, x_ref, state_ref, slope_ref):
+def gather_kernel(blocks, proj_ref, halo_ref, up_ref, weight_ref, rate_ref, x_ref, state_ref, slope_ref, pad_ref):
     size = proj_ref.shape[1]
+    zero = jnp.minimum(pl.program_id(0), 0)
+    keep = iota((LANES, 2 * LANES), 0) // GROUP == iota((LANES, 2 * LANES), 1) % LANES // GROUP
+    tables = [
+        [halves(source) for source in decay_table(rate_ref[block], size)] for block in range(blocks)
+    ]
+    pairs = []
     for block in range(blocks):
         lanes = pl.ds(block * LANES, LANES)
-        (query, key, value), _ = features_of(proj_ref, halo_ref, weight_ref, lanes)
+        (query, key, value), _ = features_of(proj_ref, halo_ref, weight_ref, pad_ref.at[block], lanes, zero)
         gated = (key * value).astype(jnp.bfloat16)
         grad = (up_ref[:, lanes].astype(jnp.float32) * query).astype(jnp.bfloat16)
-        turned = dot(flip_matrix(size), grad).astype(jnp.bfloat16)
-        both = jnp.concatenate([gated, turned], axis=1)
-        x_ref[block] = both
-        table, slope = decay_table(rate_ref[block], size)
-        keep = iota((LANES, 2 * LANES), 0) // GROUP == iota((LANES, 2 * LANES), 1) % LANES // GROUP
-        for source, target in ((table, state_ref), (slope, slope_ref)):
-            high, low = halves(source)
-            full = dot(high, both, ((0,), (0,))) + dot(low, both, ((0,), (0,)))
+        pairs.append((gated, grad))
+    boths = []
+    for block in range(blocks):
+        gated, grad = pairs[block]
+        boths.append(jnp.concatenate([gated, dot(flip_matrix(size), grad).astype(jnp.bfloat16)], axis=1))
+        x_ref[block] = boths[-1]
+    for block in range(blocks):
+        for (high, low), target in zip(tables[block], (state_ref, slope_ref)):
+            full = dot(
+                jnp.concatenate([high, low], axis=0),
+                jnp.concatenate([boths[block], boths[block]], axis=0),
+                ((0,), (0,)),
+            )
             full = jnp.where(keep, full, 0.0)
             target[block] = jnp.sum(full.reshape(PER_BLOCK, GROUP, 2 * LANES), axis=0)
 
@@ -108,6 +122,7 @@
     size = x_ref.shape[1]
     runs = size // SUB
     small_keep = iota((PER_BLOCK, LANES), 0) == iota((PER_BLOCK, LANES), 1) // GROUP
+    wide_keep = iota((PER_BLOCK, 2 * LANES), 0) == iota((PER_BLOCK, 2 * LANES), 1) % LANES // GROUP
     lag_lane = iota((PER_BLOCK, LANES), 1)
     lag_seat = iota((PER_BLOCK, LANES), 0) % runs
     keep = (
@@ -123,7 +138,15 @@
     for block in every:
         forward = jnp.exp(-(rate_ref[base + block] * steps))
         spread = jnp.where(small_keep, jnp.broadcast_to(gain_ref[base + block], (PER_BLOCK, LANES)), 0.0)
-        taps.append(dot(spread, forward, ((1,), (1,)), PRECISE))
+        a, b, c = thirds(spread)
+        d, e, f = thirds(forward)
+        taps.append(
+            dot(
+                jnp.concatenate([a, a, b, a, b, c], axis=1),
+                jnp.concatenate([d, e, d, f, e, d], axis=1),
+                ((1,), (1,)),
+            )
+        )
     chosen = []
     for block in every:
         picks = []
@@ -183,12 +206,18 @@
             inside = (lag_lane >= begin) & (lag_lane < begin + 2 * SUB - 1)
             total = total + jnp.where(inside, lines, 0.0)
         lags.append(total)
-    spreads = [[dot(lags[block], source, precision=PRECISE) for source in tables[block]] for block in every]
     for block in every:
-        outs = [
-            jnp.sum(jnp.where(small_keep, spread, 0.0), axis=0, keepdims=True) for spread in spreads[block]
-        ]
-        mode_ref[base + block] = jnp.concatenate(outs + [jnp.zeros((6, LANES), jnp.float32)], axis=0)
+        high, low = halves(lags[block])
+        table_high, table_low = halves(jnp.concatenate(tables[block], axis=1))
+        spread = dot(
+            jnp.concatenate([high, high, low], axis=1),
+            jnp.concatenate([table_high, table_low, table_high], axis=0),
+        )
+        spread = jnp.where(wide_keep, spread, 0.0)
+        line = jnp.sum(spread, axis=0, keepdims=True)
+        mode_ref[base + block] = jnp.concatenate(
+            [line[:, :LANES], line[:, LANES:], jnp.zeros((6, LANES), jnp.float32)], axis=0
+        )
 
 
 def scan_states(size, ctx, count, recv_ref, rate_ref, carry_ref, extra_ref):
@@ -277,7 +306,7 @@
 def outer_kernel(
     counts, blocks, norm, proj_ref, halo_ref, up_ref, weight_ref, skip_ref, rate_ref, gain_ref, y_ref,
     carry_ref, slope_ref, mode_ref, extra_ref, mixed_ref, grad_ref, after_ref, last_ref, out_ref,
-    part_ref, head_ref, next_ref, near_ref, sum_ref, far_ref, done_ref, all_ref,
+    pad_ref, tail_ref, part_ref, head_ref, next_ref, near_ref, sum_ref, far_ref, done_ref, all_ref,
     send_one, recv_one, send_two, recv_two, send_three, recv_three, send_head, recv_head,
 ):
     dp_count, ctx_count, tp_count = counts
@@ -305,20 +334,25 @@
         for pair in others:
             pl.semaphore_signal(barrier, inc=1, device_id=cross(pair), device_id_type=MESH)
 
-    row = iota((size, LANES), 0)
+    zero = jnp.minimum(index, 0)
     keep = iota((LANES, 2 * LANES), 0) // GROUP == iota((LANES, 2 * LANES), 1) % LANES // GROUP
     ages = (iota((size, LANES), 0) + 1).astype(jnp.float32)
     for block in range(blocks):
         lanes = pl.ds(block * LANES, LANES)
-        (query, key, value), taps = features_of(proj_ref, halo_ref, weight_ref, lanes)
+        (query, key, value), taps = features_of(proj_ref, halo_ref, weight_ref, pad_ref.at[block], lanes, zero)
         gated = (key * value).astype(jnp.bfloat16).astype(jnp.float32)
         rate_row = rate_ref[block]
         coef = gain_ref[block] * jnp.exp(-(rate_row * ages))
         coef_high, coef_low = halves(coef)
         carry = carry_ref[block]
-        spread = jnp.where(keep, jnp.concatenate([carry] * PER_BLOCK, axis=0), 0.0)
-        high, low = halves(spread)
-        whole = y_ref[block] + (dot(coef_high, high) + (dot(coef_high, low) + dot(coef_low, high)))
+        high, low = (
+            jnp.where(keep, jnp.concatenate([value] * PER_BLOCK, axis=0), jnp.zeros((), jnp.bfloat16))
+            for value in halves(carry)
+        )
+        whole = y_ref[block] + dot(
+            jnp.concatenate([coef_high, coef_high, coef_low], axis=1),
+            jnp.concatenate([high, low, high], axis=0),
+        )
         narrow = whole.astype(jnp.bfloat16)
         convolved = narrow[:, :LANES].astype(jnp.float32)
         correlated = dot(flip_matrix(size), narrow[:, LANES:])
@@ -333,8 +367,10 @@
         lasts = []
         for part, grads in enumerate((upstream * mixture, grad_gate * value, grad_gate * key)):
             weight = weight_ref[part, :, lanes]
-            ahead = jnp.where(row < size - 1, pltpu.roll(grads, size - 1, 0), 0.0)
-            further = jnp.where(row < size - 2, pltpu.roll(grads, size - 2, 0), 0.0)
+            tail_ref[block, part, :size] = grads
+            tail_ref[block, part, size:] = jnp.zeros((8, LANES), jnp.float32)
+            ahead = tail_ref[block, part, pl.ds(zero + 1, size)]
+            further = tail_ref[block, part, pl.ds(zero + 2, size)]
             result = grads * weight[0:1] + ahead * weight[1:2] + further * weight[2:3]
             grad_ref[part, :, lanes] = result.astype(jnp.bfloat16)
             heads.append(grads[:2])
@@ -466,6 +502,7 @@
     own_blocks = block_count // ctx_count
     group_count = width // GROUP
     blocks = math.gcd(block_count, 4)
+    wide_blocks = math.gcd(block_count, 8)
     norm = 1.0 / math.sqrt(dp_count * ctx_count * size)
 
     proj = projected[0].transpose(1, 0, 2)
@@ -507,6 +544,7 @@
             array(block_count, GROUP, 2 * LANES),
             array(block_count, GROUP, 2 * LANES),
         ],
+        scratch_shapes=[pltpu.VMEM((blocks, 3, size + 8, LANES), jnp.float32)],
         compiler_params=params,
         name="states",
     )(proj, before, up, short_weight, rate_rows)
@@ -514,7 +552,7 @@
     vmem = pl.BlockSpec(memory_space=pltpu.VMEM)
     table = (ctx_count, own_blocks, GROUP, 2 * LANES)
     y, modes, carry, extra = pl.pallas_call(
-        functools.partial(exchange_kernel, ctx_count, blocks, block_count // blocks // 2),
+        functools.partial(exchange_kernel, ctx_count, wide_blocks, block_count // wide_blocks // 2),
         in_specs=[vmem] * 5,
         out_specs=[vmem] * 4,
         out_shape=[
@@ -577,6 +615,8 @@
             array(ctx_count, *own),
         ],
         scratch_shapes=[
+            pltpu.VMEM((blocks, 3, size + 8, LANES), jnp.float32),
+            pltpu.VMEM((blocks, 3, size + 8, LANES), jnp.float32),
             pltpu.VMEM((ctx_count,) + own, jnp.float32),
             pltpu.VMEM((rounds, 8, step_width), jnp.float32),
             pltpu.VMEM((rounds, 8, step_width), jnp.float32),

time: 89.3 us -> 86.5 us (0.969)
  Pallas kernels: 77.3 us -> 74.5 us
    pallas_call x1, Pallas kernels: 10.4 us -> 8.55 us  [local(): pl.pallas_call(functools.partial(gather_kernel, blocks), grid=grid, in_sp...]
where the time goes in v4:
time: 86.5 us; the launch traced here: 85.9 us
  Pallas kernels  74.5 us (86%)
  local copies, waits for them, and re-layouts  4.76 us (6%)
  starting transfers between devices  4.5 us (5%)
  other arithmetic  1.41 us (2%)
    pallas_call x1, Pallas kernels, local(): pl.pallas_call(functools.partial(outer_kernel, (dp_count, ctx_count, tp_c...  34 us
    pallas_call x1, Pallas kernels, local(): pl.pallas_call(functools.partial(exchange_kernel, ctx_count, wide_blocks,...  25 us
    pallas_call x1, Pallas kernels, local(): pl.pallas_call(functools.partial(gather_kernel, blocks), grid=grid, in_sp...  8.55 us
    pallas_call x1, Pallas kernels, local(): pl.pallas_call(functools.partial(finish_kernel, blocks), grid=grid, in_sp...  6.89 us
    ppermute x1, starting transfers between devices, shifted(): lax.ppermute(value, axis, [(source, source + steps) for source in range(l...  4.5 us
  transfers between devices with their start and end apart: 1, of which 0 were waited for; matrix products, arithmetic and copies ran while one was open for 3% of the time, Pallas kernels for 0%

profile of v4, /device:TPU:1, one launch (start us, length us, event | category | flops | bytes accessed | tf_op | source)
XLA Modules:
  0.0 85.9 jit_solution(5865050434742405120)
XLA Ops:
  0.6 1.0 %slice.16 = bf16[3,2,4096]{2,1,0:T(2,128)(2,1)S(1)} slice(bf16[3,128,4096]{2,1,0:T(8,128)(2,1)} %bitcast.26), slice={[0:3], [126:128], [0:4096]} | slice | bytes 98304 | tf_op jit(solution)/shard_map/slice | solution.py:510
  1.6 4.5 %collective-permute-start = (bf16[3,2,4096]{2,1,0:T(2,128)(2,1)S(1)}, bf16[3,2,4096]{2,1,0:T(2,128)(2,1)S(1)}, u32[]{:S(2)}, u32[]{:S(2)}) collective-permute-start(bf16[3,2,4096]{2,1,0:T(2,128)(2,1)S(1)} %slice.16), channel_id=1, source_target_pairs={{0,2},{2,4},{4,6},{6,8},{8,10},{10,12},{12,14},{14,16},{16,18},{18... | collective-permute-start | bytes 147464 | tf_op jit(solution)/shard_map/ppermute | solution.py:22
  6.1 0.7 sqrt_multiply_fusion.3
  6.9 0.1 copy.32
  7.0 0.1 reshape.43
  7.1 0.0 copy-start
  7.1 0.6 constant_dynamic-slice_fusion.own_ref
  7.7 0.1 copy.33
  7.8 0.7 reshape.44
  8.5 0.0 collective-permute-done.halo_ref
  8.5 0.0 copy-start.1
  8.5 0.0 copy-done
  8.5 0.6 copy-done.1
  9.1 8.5 %states.1 = (bf16[32,128,256]{2,1,0:T(8,128)(2,1)}, f32[32,16,256]{2,1,0:T(8,128)}, f32[32,16,256]{2,1,0:T(8,128)}) custom-call(bf16[3,128,4096]{2,1,0:T(8,128)(2,1)} %bitcast.27, bf16[3,2,4096]{2,1,0:T(2,128)(2,1)} %copy-done.1, bf16[128,4096]{1,0:T(8,128)(2,1)} %bitcast.29, f32[3,3,4096]{2,1,0:T(4,128)} %weight_ref.5, f32[32,1,128]{2,1,0:T(1,128)} %bitcast.39), custom_call_target="tpu_custom_call" | custom-call | tf_op jit(solution)/shard_map/states/pallas_call | solution.py:537
  17.7 25.0 %exchange.1 = (f32[32,128,256]{2,1,0:T(8,128)}, f32[32,8,128]{2,1,0:T(8,128)}, f32[16,2,16,256]{3,2,1,0:T(8,128)}, f32[2,16,128]{2,1,0:T(8,128)}) custom-call(f32[16,2,16,256]{3,2,1,0:T(8,128)} %bitcast.35, bf16[32,128,256]{2,1,0:T(8,128)(2,1)} %get-tuple-element.23.x_ref, f32[32,1,128]{2,1,0:T(1,128)} %bitcast.40, f32[32,1,128]{2,1,0:T(1,128)} %bitcast.42, ...), custom_call_target="tpu_custom_call" | custom-call | tf_op jit(solution)/shard_map/exchange/pallas_call | solution.py:554
  42.7 0.0 copy-start.2
  42.7 0.0 copy-start.3
  42.7 34.0 %outer.1 = (bf16[128,4096]{1,0:T(8,128)(2,1)}, bf16[3,128,4096]{2,1,0:T(8,128)(2,1)}, f32[8,4096]{1,0:T(8,128)}, f32[8,4096]{1,0:T(8,128)}, f32[16,2,16,128]{3,2,1,0:T(8,128)}) custom-call(bf16[3,128,4096]{2,1,0:T(8,128)(2,1)} %bitcast.28, bf16[3,2,4096]{2,1,0:T(2,128)(2,1)} %copy-done.1, bf16[128,4096]{1,0:T(8,128)(2,1)} %bitcast.30, ...), custom_call_target="tpu_custom_call" | custom-call | tf_op jit(solution)/shard_map/outer/pallas_call | solution.py:598
  76.7 0.9 %slice.17 = f32[32,4,128]{2,1,0:T(4,128)S(1)} slice(f32[32,16,128]{2,1,0:T(8,128)} %bitcast.36), slice={[0:32], [10:14], [0:128]} | slice | bytes 131072 | tf_op jit(solution)/shard_map/slice | solution.py:660
  77.6 0.1 copy.40
  77.8 0.1 copy.44
  78.0 0.1 copy.45
  78.0 0.2 copy.41
  78.2 0.1 copy.42
  78.3 0.0 copy-done.2
  78.3 0.0 copy-done.3
  78.3 0.7 fusion.4
  79.0 6.9 %finish.1 = (bf16[3,128,4096]{2,1,0:T(8,128)(2,1)}, bf16[128,4096]{1,0:T(8,128)(2,1)}, f32[3,3,4096]{2,1,0:T(4,128)}, f32[1,4096]{1,0:T(1,128)}) custom-call(bf16[3,128,4096]{2,1,0:T(8,128)(2,1)} %get-tuple-element.29.grad_ref, bf16[128,4096]{1,0:T(8,128)(2,1)} %get-tuple-element.30.mixed_ref, f32[8,4096]{1,0:T(8,128)} %get-tuple-element.31.after_ref, ...), custom_call_target="tpu_custom_call" | custom-call | tf_op jit(solution)/shard_map/finish/pallas_call | solution.py:645
  (1 shorter events, 0.0 us)
Async XLA Ops:
  1.6 6.9 %collective-permute-start = (bf16[3,2,4096]{2,1,0:T(2,128)(2,1)S(1)}, bf16[3,2,4096]{2,1,0:T(2,128)(2,1)S(1)}, u32[]{:S(2)}, u32[]{:S(2)}) collective-permute-start(bf16[3,2,4096]{2,1,0:T(2,128)(2,1)S(1)} %slice.16), channel_id=1, source_target_pairs={{0,2},{2,4},{4,6},{6,8},{8,10},{10,12},{12,14},{14,16},{16,18},{18... | collective-permute-start | bytes 147464 | tf_op jit(solution)/shard_map/ppermute | solution.py:22
  7.1 1.4 %copy-start = (f32[32,1,128]{2,0,1:T(8,128)}, f32[32,1,128]{2,0,1:T(8,128)S(1)}, u32[]{:S(2)}) copy-start(f32[32,1,128]{2,0,1:T(8,128)S(1)} %reshape.43) | copy-start | bytes 49156
  8.5 0.6 copy-start.1
  42.7 35.7 %copy-start.2 = (f32[512,16]{0,1:T(8,128)S(1)}, f32[512,16]{0,1:T(8,128)}, u32[]{:S(2)}) copy-start(f32[512,16]{0,1:T(8,128)} %param.10) | copy-start | bytes 98308
  42.7 35.6 %copy-start.3 = (f32[512,16]{0,1:T(8,128)S(1)}, f32[512,16]{0,1:T(8,128)}, u32[]{:S(2)}) copy-start(f32[512,16]{0,1:T(8,128)} %param.11) | copy-start | bytes 98308
